TPU v7x, 512 devices: a whole 4x4x16 slice. The times are simulated.
512 devices in a mesh: layer: 64 (over z, x), dp: 8 (over y, core).
Axes of the slice: x: 4, y: 4, z: 16, core: 2. Of those that a mesh axis runs over, the one named last changes fastest.
Arguments:
- states: float32 [64, 8, 24, 1536], P('layer', 'dp'), may hold values from -6 to 6
- adjoints: float32 [64, 8, 24, 1536], P('layer', 'dp'), may hold values from -6 to 6
- kernels: bfloat16 [256, 3, 3, 64, 64], P('layer'), may hold values from -0.25 to 0.25
- biases: float32 [256, 64], P('layer'), may hold values from -4 to 4
- coarse_gain: float32 [64, 64], P('layer'), may hold values from 0.01 to 1
Outputs:
- states_new: float32 [64, 8, 24, 1536], P('layer', 'dp')
- adjoints_new: float32 [64, 8, 24, 1536], P('layer', 'dp')
- kernel_grad: float32 [256, 3, 3, 64, 64], P('layer')
- bias_grad: float32 [256, 64], P('layer')
All inputs are finite; a program needn't handle non-finite values.
Results may differ from a plain program's by a relative error of at most 0.0054.
Values sent between devices are 32-bit elements; how exact they have to be, the bound alone decides.
No kernel may reach another device: no remote copies, remote signals or barrier semaphores. Data moves between devices by JAX's collectives and lax.ppermute only.
A program may use at most 64 MiB of HBM per device.

v0:
```python
import jax
import jax.numpy as jnp
from jax import lax
from jax.sharding import PartitionSpec as P

step_size = 0.5


def prefix(array, axis, combine, identity, reverse):
    length, position = (lax.axis_size(axis), lax.axis_index(axis))
    everything = jax.tree.map(lambda part: lax.all_gather(part, axis), array)
    start = jax.tree.map(
        lambda part, zero: jnp.broadcast_to(jnp.asarray(zero, part.dtype), part.shape),
        array,
        identity,
    )

    def turn(k, before):
        at = length - 1 - k if reverse else k
        reached = at > position if reverse else at < position
        new = combine(before, jax.tree.map(lambda part: part[at], everything))
        return jax.tree.map(lambda a, b: jnp.where(reached, a, b), new, before)

    return lax.fori_loop(0, length, turn, start)


def correlate(field, kernel):
    return lax.conv_general_dilated(
        field,
        kernel,
        (1, 1),
        "SAME",
        dimension_numbers=("NHWC", "HWIO", "NHWC"),
        preferred_element_type=jnp.float32,
    )


def kernel_terms(field, sens_round):
    rows_img = field.shape[1]
    cols_img = field.shape[2]
    channels = field.shape[3]
    padded = jnp.pad(field.astype(jnp.bfloat16), ((0, 0), (1, 1), (1, 1), (0, 0)))
    flat_sens = sens_round.reshape(-1, channels)
    terms = []
    for row in range(3):
        for col in range(3):
            piece = padded[:, row : row + rows_img, col : col + cols_img].reshape(-1, channels)
            terms.append(
                lax.dot_general(
                    piece, flat_sens, (((0,), (0,)), ((), ())), preferred_element_type=jnp.float32
                )
            )
    return jnp.stack(terms).reshape(3, 3, channels, channels)


def compose(earlier, later):
    return (earlier[0] * later[0], later[0] * earlier[1] + later[1])


def body(states, adjoints, kernels, biases, coarse_gain):
    count_img, rows_img, flat = (states.shape[1], states.shape[2], states.shape[3])
    channels = kernels.shape[-1]
    cols_img = flat // channels
    shape_four = (count_img, rows_img, cols_img, channels)
    position = lax.axis_index("layer")
    block_count = lax.axis_size("layer")
    images = count_img * lax.axis_size("dp")
    depth_count = kernels.shape[0]
    field = states[0].reshape(shape_four)
    path = []
    acts = []
    for depth in range(depth_count):
        activ = jnp.tanh(correlate(field.astype(jnp.bfloat16), kernels[depth]) + biases[depth])
        path.append(field)
        acts.append(activ)
        field = field + step_size * activ
    gain_row = jnp.tile(coarse_gain[0], cols_img).reshape(1, 1, flat)
    zero_row = jnp.zeros_like(gain_row)
    lead_gain = jnp.where(position == 0, zero_row, gain_row)
    offset = field.reshape(count_img, rows_img, flat) - lead_gain * states[0]
    identity = (jnp.ones_like(gain_row), jnp.zeros_like(offset))
    prefix_gain, prefix_sum = prefix((lead_gain, offset), "layer", compose, identity, False)
    states_new = (prefix_gain * states[0] + prefix_sum)[None]
    adjoint = adjoints[0].reshape(shape_four)
    kgrads = [None] * depth_count
    bgrads = [None] * depth_count
    for depth in reversed(range(depth_count)):
        sens = step_size * (1.0 - acts[depth] * acts[depth]) * adjoint
        sens_round = sens.astype(jnp.bfloat16)
        flipped = kernels[depth][::-1, ::-1].transpose(0, 1, 3, 2)
        adjoint = adjoint + correlate(sens_round, flipped)
        kernel_term = kernel_terms(path[depth], sens_round)
        bias_term = jnp.sum(sens, axis=(0, 1, 2))
        kgrads[depth] = kernel_term
        bgrads[depth] = bias_term
    kernel_grad = jnp.stack(kgrads)
    bias_grad = jnp.stack(bgrads)
    kernel_grad, bias_grad = lax.psum((kernel_grad, bias_grad), "dp")
    tail_gain = jnp.where(position == block_count - 1, zero_row, gain_row)
    tail_offset = adjoint.reshape(count_img, rows_img, flat) - tail_gain * adjoints[0]
    suffix_gain, suffix_sum = prefix((tail_gain, tail_offset), "layer", compose, identity, True)
    adjoints_new = (tail_gain * suffix_sum + tail_offset)[None]
    return (states_new, adjoints_new, kernel_grad / images, bias_grad / images)


def solution(mesh):
    return jax.shard_map(
        body,
        mesh=mesh,
        in_specs=(
            P("layer", "dp", None, None),
            P("layer", "dp", None, None),
            P("layer", None, None, None, None),
            P("layer", None),
            P("layer", None),
        ),
        out_specs=(
            P("layer", "dp", None, None),
            P("layer", "dp", None, None),
            P("layer", None, None, None, None),
            P("layer", None),
        ),
        check_vma=False,
    )
```

profile of v0, /device:TPU:8, one launch (start us, length us, event | category | flops | bytes accessed | tf_op | source)
XLA Modules:
  0.0 436.1 jit_solution(16834524327577105897)
XLA Ops:
  8.1 1.1 reshape_squeeze.6
  11.1 1.2 subtract_multiply_fusion.2
  14.7 1.2 subtract_multiply_fusion
  34.4 1.1 pad_maximum_fusion
  36.4 1.5 convolution_select_fusion
  39.5 14.7 %psum.15 = f32[4,64]{1,0:T(4,128)S(1)} all-reduce(f32[4,64]{1,0:T(4,128)S(1)} %pad_maximum_fusion.1), channel_id=1, replica_groups=mesh['layer'=64,'dp'=8] {'dp'}, use_global_device_ids=true, to_apply=%region_9.10 | all-reduce | flops 256 | bytes 2048 | tf_op jit(solution)/shard_map/psum | solution.py:98
  54.9 98.9 %all_gather.16 = f32[64,1,1,1536]{3,2,1,0:T(1,128)S(1)} all-gather(f32[1,1,1,1536]{3,2,1,0:T(1,128)S(1)} %select_n.132), channel_id=1, replica_groups=mesh['layer'=64,'dp'=8] {'layer'}, dimensions={0}, use_global_device_ids=true | all-gather | bytes 399360 | tf_op jit(solution)/shard_map/all_gather | solution.py:11
  153.8 93.8 %all_gather.18 = f32[64,1,1,1536]{3,2,1,0:T(1,128)S(1)} all-gather(f32[1,1,1,1536]{3,2,1,0:T(1,128)S(1)} %select_n.138), channel_id=1, replica_groups=mesh['layer'=64,'dp'=8] {'layer'}, dimensions={0}, use_global_device_ids=true | all-gather | bytes 399360 | tf_op jit(solution)/shard_map/all_gather | solution.py:11
  247.6 2.4 broadcast_multiply_fusion
  250.0 68.7 %while.32 = (s32[]{:T(128)}, f32[1,1,1536]{2,1,0:T(1,128)S(1)}, f32[1,24,1536]{2,1,0:T(8,128)S(1)}, s32[]{:T(128)}, f32[64,1,1,1536]{3,2,1,0:T(1,128)S(1)}, /*in...) while((s32[]{:T(128)}, f32[1,1,1536]{2,1,0:T(1,128)S(1)}, f32[1,24,1536]{2,1,0:T(8,128)S(1)}, ...), condition=%wide.region_1.2_spmd.clone, body=%wide.region_0.1_spmd.clone.sunk | while | flops 152068 | bytes 479351 | solution.py:24
  256.5 1.0 fusion.321
  257.6 1.0 fusion.321
  260.8 1.0 fusion.321
  265.1 1.0 fusion.321
  268.3 1.0 fusion.321
  287.6 1.0 fusion.321
  288.7 1.0 fusion.321
  295.2 1.0 fusion.321
  296.2 1.0 fusion.321
  298.4 1.0 fusion.321
  301.6 1.0 fusion.321
  304.8 1.0 fusion.321
  311.3 1.0 fusion.321
  312.3 1.0 fusion.321
  314.5 1.0 fusion.321
  315.6 1.0 fusion.321
  318.7 41.4 %all-gather.5.cloned.1.call-done = f32[64,1,24,1536]{3,2,1,0:T(8,128)} async-done(((f32[1,1,24,1536]{3,2,1,0:T(8,128)}), f32[64,1,24,1536]{3,2,1,0:T(8,128)}) %all-gather.5.cloned.1.call-update) | async-done | bytes 9437200 | tf_op jit(solution)/shard_map/all_gather | solution.py:11
  360.1 67.7 %while.33 = (s32[]{:T(128)}, f32[1,24,1536]{2,1,0:T(8,128)S(1)}, s32[]{:T(128)}, f32[64,1,1,1536]{3,2,1,0:T(1,128)S(1)}, f32[64,1,24,1536]{3,2,1,0:T(8,128)}, /*index=5*/s32[]{:T(128)}, s32[]{:T(128)}, s32[]{:T(128)}, s32[]{:T(128)}) while((s32[]{:T(128)}, f32[1,24,1536]{2,1,0:T(8,128)S(1)}, s32[]{:T(128)}, ...), condition=%wide.region_3.4_spmd.clone, body=%wide.region_2.3_spmd.clone.sunk | while | flops 147464 | bytes 460967 | solution.py:24
  361.2 1.0 fusion.322
  362.3 1.0 fusion.322
  364.4 1.0 fusion.322
  367.6 1.0 fusion.322
  (470 shorter events, 137.6 us)
Async XLA Ops:
  8.0 2.1 copy-start.15
  8.0 2.0 copy-start.10
  8.0 2.1 copy-start.12
  8.0 239.6 %all-reduce.6.cloned.1.call-start = ((), (), s32[]{:S(2)}) async-start(), calls=%async_computation.2 | async-start | bytes 2359296 | tf_op jit(solution)/shard_map/psum | solution.py:98
  12.6 1.1 copy-start.13
  15.9 0.9 copy-start
  16.9 1.1 copy-start.14
  20.4 1.0 copy-start.3
  23.7 0.9 copy-start.8
  24.2 1.4 copy-start.2
  25.5 0.7 copy-start.6
  25.8 0.7 copy-start.11
  25.8 0.9 copy-start.1
  26.4 1.2 copy-start.7
  26.4 1.4 copy-start.9
  27.4 1.3 copy-start.5
  29.2 1.4 copy-start.4
  35.6 214.4 %all-gather.3.cloned.1.call-start = ((), (), s32[]{:S(2)}) async-start(), calls=%async_computation | async-start | bytes 9584640 | tf_op jit(solution)/shard_map/all_gather | solution.py:11
  36.2 323.9 %all-gather.5.cloned.1.call-start = ((), (), s32[]{:S(2)}) async-start(), calls=%async_computation.1 | async-start | bytes 9584640 | tf_op jit(solution)/shard_map/all_gather | solution.py:11
Sparse Core Ops, SparseCore 0:
  35.7 81.4 all-reduce.5
Sparse Core Ops, SparseCore 1:
  39.6 164.0 all-gather.2
  207.1 153.0 all-gather.4
where the time goes:
time: 439 us; the launch traced here: 436 us
  blocking collectives  207 us (47%)
  other arithmetic  136 us (31%)
  waiting for transfers between devices  41.9 us (10%)
  between operations  16.4 us (4%)
  matrix products  16.2 us (4%)
  local copies, waits for them, and re-layouts  12.9 us (3%)
  loops' own time  4.68 us (1%)
    all_gather x2, blocking collectives, prefix(): everything = jax.tree.map(lambda part: lax.all_gather(part, axis), array)  193 us
    select_n x192, other arithmetic, turn(): return jax.tree.map(lambda a, b: jnp.where(reached, a, b), new, before)  128 us
    all_gather x2, waiting for transfers between devices, prefix(): everything = jax.tree.map(lambda part: lax.all_gather(part, axis), array)  41.4 us
    psum x1, blocking collectives, body(): kernel_grad, bias_grad = lax.psum((kernel_grad, bias_grad), 'dp')  14.7 us
    dot_general x36, matrix products, kernel_terms(): lax.dot_general(piece, flat_sens, (((0,), (0,)), ((), ())), preferred_ele...  9.39 us
  transfers between devices with their start and end apart: 3, of which 1 were waited for; matrix products, arithmetic and copies ran while one was open for 17% of the time, Pallas kernels for 0%

commit v1 on v0

v1 whole, which is shorter than its diff:
```python
import functools

import jax
import jax.numpy as jnp
from jax import lax
from jax.experimental import pallas as pl
from jax.experimental.pallas import tpu as pltpu
from jax.sharding import PartitionSpec as P

STEP = 0.5
BF = jnp.bfloat16
F32 = jnp.float32
VMEM_BYTES = 12 * 1024 * 1024


def low_lanes(rows):
    return lax.broadcasted_iota(jnp.int32, (rows, 128), 1) < 64


def to_tiles(x):
    return jnp.concatenate([x[:, 128 * k : 128 * k + 128] for k in range(x.shape[1] // 128)], axis=0)


def patches(v, rows_img):
    count = v.shape[0]
    turned = pltpu.roll(v, 64, 1)
    edge = jnp.zeros((rows_img, 128), F32)
    mid = jnp.where(
        low_lanes(count + rows_img),
        jnp.concatenate([edge, turned], axis=0),
        jnp.concatenate([turned, edge], axis=0),
    )
    total = count + rows_img
    groups = total // rows_img
    where_y = lax.broadcasted_iota(jnp.int32, (groups, rows_img, 128), 1)
    up = pltpu.roll(mid, 1, 0).reshape(groups, rows_img, 128)
    up = jnp.where(where_y == 0, 0.0, up).reshape(total, 128)
    down = pltpu.roll(mid, total - 1, 0).reshape(groups, rows_img, 128)
    down = jnp.where(where_y == rows_img - 1, 0.0, down).reshape(total, 128)
    parts = []
    for t in (up, mid, down):
        parts.append(t[:count].astype(BF))
        parts.append(t[rows_img:].astype(BF))
    return jnp.concatenate(parts, axis=1)


def forward_weights(k_ref, layer):
    zero = jnp.zeros((64, 64), BF)
    rows = []
    for dy in range(3):
        tap = [k_ref[layer * 9 + dy * 3 + dx] for dx in range(3)]
        rows.append(jnp.concatenate([tap[0], zero], axis=1))
        rows.append(jnp.concatenate([tap[1], tap[0]], axis=1))
        rows.append(jnp.concatenate([tap[2], tap[1]], axis=1))
        rows.append(jnp.concatenate([zero, tap[2]], axis=1))
    return jnp.concatenate(rows, axis=0)


def backward_weights(k_ref, layer):
    zero = jnp.zeros((64, 64), BF)
    first, second = [], []
    for dy in range(3):
        tap = [k_ref[layer * 9 + (2 - dy) * 3 + dx] for dx in range(3)]
        first += [tap[2], tap[1], tap[0], zero]
        second += [zero, tap[2], tap[1], tap[0]]
    return jnp.concatenate(
        [jnp.concatenate(first, axis=1), jnp.concatenate(second, axis=1)], axis=0
    )


def pack(out_ref, value, gain):
    for r in range(4):
        out_ref[pl.ds(r, 64, stride=5), :] = value[64 * r : 64 * r + 64]
    low = low_lanes(32)
    rest = value[256:288]
    spread = jnp.broadcast_to(gain, (32, 128))
    extra = jnp.concatenate(
        [jnp.where(low, rest, spread), jnp.where(low, pltpu.roll(rest, 64, 1), spread)], axis=0
    )
    out_ref[pl.ds(4, 64, stride=5), :] = extra


def unpack(ref):
    extra = ref[pl.ds(4, 64, stride=5), :]
    rest = jnp.where(low_lanes(32), extra[:32], pltpu.roll(extra[32:], 64, 1))
    return jnp.concatenate([ref[pl.ds(r, 64, stride=5), :] for r in range(4)] + [rest], axis=0)


def from_tiles(out_ref, value, rows_img):
    for k in range(value.shape[0] // rows_img):
        out_ref[:, 128 * k : 128 * k + 128] = value[rows_img * k : rows_img * k + rows_img]


def doubled(row):
    return jnp.concatenate([row, row], axis=1)


def forward_kernel(depth_count, st_ref, k_ref, b_ref, g_ref, send_ref, act_ref, patch_ref):
    rows_img = st_ref.shape[0]
    start = to_tiles(st_ref[...])
    field = start
    bias = doubled(b_ref[...])
    for layer in range(depth_count):
        cells = patches(field, rows_img)
        patch_ref[layer] = cells
        total = jnp.dot(cells, forward_weights(k_ref, layer), preferred_element_type=F32)
        act = jnp.tanh(total + bias[layer : layer + 1])
        act_ref[layer] = act
        field = field + STEP * act
    gain = doubled(g_ref[...])
    gain = jnp.where(lax.axis_index("layer") == 0, jnp.zeros_like(gain), gain)
    pack(send_ref, field - gain * start, gain)


def backward_kernel(depth_count, blocks, adj_ref, act_ref, k_ref, g_ref, send_ref, sens_ref, bias_ref):
    rows_img = adj_ref.shape[0]
    start = to_tiles(adj_ref[...])
    adjoint = start
    sums = [None] * depth_count
    for layer in reversed(range(depth_count)):
        act = act_ref[layer]
        sens = STEP * (1.0 - act * act) * adjoint
        sens_ref[layer] = sens.astype(BF)
        total = jnp.sum(sens, axis=0, keepdims=True)
        sums[layer] = total + pltpu.roll(total, 64, 1)
        adjoint = adjoint + lax.dot_general(
            patches(sens, rows_img),
            backward_weights(k_ref, layer),
            (((1,), (1,)), ((), ())),
            preferred_element_type=F32,
        )
    gain = doubled(g_ref[...])
    gain = jnp.where(lax.axis_index("layer") == blocks - 1, jnp.zeros_like(gain), gain)
    pack(send_ref, adjoint - gain * start, gain)
    bias_ref[...] = jnp.concatenate(sums + [jnp.zeros((8 - depth_count, 128), F32)], axis=0)


CHUNK = 144
SPAN = 152


def gradient_kernel(depth_count, patch_ref, sens_ref, bias_ref, out_ref):
    low = low_lanes(192)
    for pair in range(depth_count // 2):
        both = [
            lax.dot_general(
                patch_ref[2 * pair + q],
                sens_ref[2 * pair + q],
                (((0,), (0,)), ((), ())),
                preferred_element_type=F32,
            )
            for q in range(2)
        ]
        for dy in range(3):
            one = both[0][256 * dy : 256 * dy + 256]
            two = both[1][256 * dy : 256 * dy + 256]
            tile = jnp.where(
                low,
                one[:192] + pltpu.roll(one[64:], 64, 1),
                pltpu.roll(two[:192], 64, 1) + two[64:],
            )
            at, done = pair * 576 + dy * 192, 0
            while done < 192:
                chunk, within = (at + done) // CHUNK, (at + done) % CHUNK
                size = min(CHUNK - within, 192 - done)
                out_ref[SPAN * chunk + within : SPAN * chunk + within + size] = tile[done : done + size]
                done += size
    for chunk in range(8):
        rows = slice(SPAN * chunk + CHUNK, SPAN * chunk + SPAN)
        out_ref[rows] = bias_ref[...] if chunk == 0 else jnp.zeros((SPAN - CHUNK, 128), F32)


def total_kernel(scale, in_ref, out_ref):
    total = in_ref[0]
    for other in range(1, in_ref.shape[0]):
        total = total + in_ref[other]
    total = total * scale
    for other in range(out_ref.shape[0]):
        out_ref[other] = total


def spread_kernel(depth_count, in_ref, grad_ref, bias_ref):
    bias_ref[...] = in_ref[CHUNK : CHUNK + depth_count, :64]
    for pair in range(depth_count // 2):
        for tap in range(9):
            at = pair * 576 + tap * 64
            pieces, done = [], 0
            while done < 64:
                chunk, within = (at + done) // CHUNK, (at + done) % CHUNK
                size = min(CHUNK - within, 64 - done)
                pieces.append(in_ref[SPAN * chunk + within : SPAN * chunk + within + size])
                done += size
            tile = pieces[0] if len(pieces) == 1 else jnp.concatenate(pieces, axis=0)
            grad_ref[18 * pair + tap] = tile[:, :64]
            grad_ref[18 * pair + 9 + tap] = pltpu.roll(tile, 64, 1)[:, :64]


def scan_kernel(blocks, reverse, in_ref, out_ref):
    extra = in_ref[pl.ds(4, blocks, stride=5), :]
    gains = jnp.where(low_lanes(blocks), pltpu.roll(extra, 64, 1), extra)
    value = jnp.zeros((5, 128), F32)
    for step in range(blocks):
        at = blocks - 1 - step if reverse else step
        rows = slice(5 * at, 5 * at + 5)
        following = gains[at : at + 1] * value + in_ref[rows]
        out_ref[rows] = following if reverse else value
        value = following


def finish_kernel(rows_img, in_ref, st_ref, out_ref):
    value = unpack(in_ref)
    from_tiles(out_ref, value, rows_img)

    @pl.when(lax.axis_index("layer") == 0)
    def _():
        out_ref[...] = st_ref[...]


def finish_last_kernel(rows_img, in_ref, out_ref):
    from_tiles(out_ref, unpack(in_ref), rows_img)


def call(kernel, name, outs, *args, flops=0):
    shapes = [jax.ShapeDtypeStruct(s, d) for s, d in outs]
    size = sum(a.size * a.dtype.itemsize for a in list(args) + shapes)
    return pl.pallas_call(
        kernel,
        out_shape=shapes,
        in_specs=[pl.BlockSpec(memory_space=pltpu.VMEM)] * len(args),
        out_specs=[pl.BlockSpec(memory_space=pltpu.VMEM)] * len(outs),
        compiler_params=pltpu.CompilerParams(vmem_limit_bytes=VMEM_BYTES),
        cost_estimate=pl.CostEstimate(flops=flops, bytes_accessed=size, transcendentals=0),
        name=name,
    )(*args)


def exchange(rows, axis, count):
    moved = lax.all_to_all(rows.reshape(count, -1), axis, 0, 0, tiled=True)
    return moved.reshape(rows.shape)


def body(states, adjoints, kernels, biases, coarse_gain):
    rows_img, flat = states.shape[2:]
    depth_count = kernels.shape[0]
    blocks, parts = lax.axis_size("layer"), lax.axis_size("dp")
    tiles = rows_img * flat // 128
    state = states.reshape(rows_img, flat)
    adjoint = adjoints.reshape(rows_img, flat)
    taps = kernels.reshape(depth_count * 9, 64, 64)
    field = ((tiles, 128), F32)
    packet = ((5 * blocks, 128), F32)
    image = ((rows_img, flat), F32)
    send, acts, cells = call(
        functools.partial(forward_kernel, depth_count),
        "forward",
        [packet, ((depth_count,) + field[0], F32), ((depth_count, tiles, 768), BF)],
        state, taps, biases, coarse_gain,
        flops=depth_count * tiles * 768 * 256,
    )
    came = exchange(send, "layer", blocks)
    send_adj, sens, bias = call(
        functools.partial(backward_kernel, depth_count, blocks),
        "backward",
        [packet, ((depth_count,) + field[0], BF), ((8, 128), F32)],
        adjoint, acts, taps, coarse_gain,
        flops=depth_count * tiles * 768 * 256,
    )
    came_adj = exchange(send_adj, "layer", blocks)
    (grads,) = call(
        functools.partial(gradient_kernel, depth_count),
        "gradient",
        [((SPAN * parts, 128), F32)],
        cells, sens, bias,
        flops=depth_count * tiles * 768 * 256,
    )
    shares = lax.all_to_all(grads.reshape(parts, SPAN, 128), "dp", 0, 0, tiled=True)
    (back,) = call(functools.partial(scan_kernel, blocks, False), "scan", [packet], came)
    home = exchange(back, "layer", blocks)
    (back_adj,) = call(functools.partial(scan_kernel, blocks, True), "scan_adj", [packet], came_adj)
    home_adj = exchange(back_adj, "layer", blocks)
    (sums,) = call(
        functools.partial(total_kernel, 1.0 / parts), "total", [((parts, SPAN, 128), F32)], shares
    )
    full = lax.all_to_all(sums, "dp", 0, 0, tiled=True)
    grad, bias_grad = call(
        functools.partial(spread_kernel, depth_count),
        "spread",
        [((depth_count * 9, 64, 64), F32), ((depth_count, 64), F32)],
        full.reshape(parts * SPAN, 128),
    )
    (states_new,) = call(functools.partial(finish_kernel, rows_img), "finish", [image], home, state)
    (adjoints_new,) = call(functools.partial(finish_last_kernel, rows_img), "finish_adj", [image], home_adj)
    return (
        states_new.reshape(states.shape),
        adjoints_new.reshape(adjoints.shape),
        grad.reshape(kernels.shape),
        bias_grad,
    )


def solution(mesh):
    return jax.shard_map(
        body,
        mesh=mesh,
        in_specs=(
            P("layer", "dp", None, None),
            P("layer", "dp", None, None),
            P("layer", None, None, None, None),
            P("layer", None),
            P("layer", None),
        ),
        out_specs=(
            P("layer", "dp", None, None),
            P("layer", "dp", None, None),
            P("layer", None, None, None, None),
            P("layer", None),
        ),
        check_vma=False,
    )
```

time: 439 us -> 148 us (0.34)
  blocking collectives: 207 us -> 51.9 us
  other arithmetic: 136 us -> 0 us
  starting transfers between devices: 0.12 us -> 18.8 us
  waiting for transfers between devices: 41.9 us -> 60.3 us
  matrix products: 16.2 us -> 0 us
  between operations: 16.4 us -> 0.69 us
  Pallas kernels: 0 us -> 10.3 us
  local copies, waits for them, and re-layouts: 12.9 us -> 5.94 us
  loops' own time: 4.68 us -> 0 us
    all_gather x2 -> x0, blocking collectives: 193 us -> none  [prefix(): everything = jax.tree.map(lambda part: lax.all_gather(part, axis), array)]
    select_n x193 -> x0, other arithmetic: 128 us -> none  [the longest x192 128 us: turn(): return jax.tree.map(lambda a, b: jnp.where(reached, a, b), new, before)]
    all_to_all x0 -> x4, waiting for transfers between devices: none -> 60.3 us  [the longest x3 51.3 us: exchange(): moved = lax.all_to_all(rows.reshape(count, -1), axis, 0, 0, tiled=True)]
    all_to_all x0 -> x2, blocking collectives: none -> 51.9 us  [the longest x1 33.7 us: exchange(): moved = lax.all_to_all(rows.reshape(count, -1), axis, 0, 0, tiled=True)]
    all_gather x2 -> x0, waiting for transfers between devices: 41.4 us -> none  [prefix(): everything = jax.tree.map(lambda part: lax.all_gather(part, axis), array)]
    all_to_all x0 -> x4, starting transfers between devices: none -> 18.8 us  [the longest x3 13.8 us: exchange(): moved = lax.all_to_all(rows.reshape(count, -1), axis, 0, 0, tiled=True)]
    psum x1 -> x0, blocking collectives: 14.7 us -> none  [body(): kernel_grad, bias_grad = lax.psum((kernel_grad, bias_grad), 'dp')]
    pallas_call x0 -> x9, Pallas kernels: none -> 10.3 us  [call(): pl.pallas_call(kernel, out_shape=shapes, in_specs=[pl.BlockSpec(memory_sp...]
  transfers between devices with their start and end apart: 3 -> 4, of which waited for: 1 -> 4; matrix products, arithmetic and copies ran while one was open for 17% -> 0% of each run, Pallas kernels for 0% -> 3%
where the time goes in v1:
time: 148 us
  waiting for transfers between devices  60.3 us (41%)
  blocking collectives  51.9 us (35%)
  starting transfers between devices  18.8 us (13%)
  Pallas kernels  10.3 us (7%)
  local copies, waits for them, and re-layouts  5.94 us (4%)
    all_to_all x3, waiting for transfers between devices, exchange(): moved = lax.all_to_all(rows.reshape(count, -1), axis, 0, 0, tiled=True)  51.3 us
    all_to_all x1, blocking collectives, exchange(): moved = lax.all_to_all(rows.reshape(count, -1), axis, 0, 0, tiled=True)  33.7 us
    all_to_all x1, blocking collectives, body(): lax.all_to_all(grads.reshape(parts, SPAN, 128), 'dp', 0, 0, tiled=True)  18.1 us
    all_to_all x3, starting transfers between devices, exchange(): moved = lax.all_to_all(rows.reshape(count, -1), axis, 0, 0, tiled=True)  13.8 us
    pallas_call x9, Pallas kernels, call(): pl.pallas_call(kernel, out_shape=shapes, in_specs=[pl.BlockSpec(memory_sp...  10.3 us
    all_to_all x1, waiting for transfers between devices, body(): full = lax.all_to_all(sums, 'dp', 0, 0, tiled=True)  9.07 us
    unnamed x16, local copies, waits for them, and re-layouts  5.94 us
    all_to_all x1, starting transfers between devices, body(): full = lax.all_to_all(sums, 'dp', 0, 0, tiled=True)  4.91 us
  transfers between devices with their start and end apart: 4, of which 4 were waited for; matrix products, arithmetic and copies ran while one was open for 0% of the time, Pallas kernels for 3%

profile of v1, /device:TPU:8, one launch (start us, length us, event | category | flops | bytes accessed | tf_op | source)
XLA Modules:
  0.0 147.9 jit_solution(5638104709076490921)
XLA Ops:
  0.6 0.0 copy-start
  0.6 1.1 copy-done
  1.7 0.0 copy-start.3
  1.7 0.9 copy-done.3
  2.6 0.0 copy-start.5
  2.6 0.7 copy-done.5
  3.3 0.0 copy-start.7
  3.3 0.7 copy-done.7
  3.9 1.8 %forward.1 = (f32[320,128]{1,0:T(8,128)S(1)}, f32[4,288,128]{2,1,0:T(8,128)S(1)}, bf16[4,288,768]{2,1,0:T(8,128)(2,1)S(1)}) custom-call(f32[24,1536]{1,0:T(8,128)S(1)} %bitcast.26, bf16[36,64,64]{2,1,0:T(8,128)(2,1)S(1)} %bitcast.22, f32[4,64]{1,0:T(4,128)S(1)} %copy-done.7, f32[1,64]{1,0:T(1,128)S(1)} %copy-done.5), custom_call_target="tpu_custom_call" | custom-call | flops 226492416 | bytes 2966784 | tf_op jit(solution)/shard_map/forward/pallas_call | solution.py:226
  5.7 0.0 copy-start.1
  5.7 1.1 copy-done.1
  6.8 0.9 copy-done.2
  7.7 0.7 copy-done.6
  8.4 2.2 %backward.1 = (f32[320,128]{1,0:T(8,128)}, bf16[4,288,128]{2,1,0:T(8,128)(2,1)S(1)}, f32[8,128]{1,0:T(8,128)S(1)}) custom-call(f32[24,1536]{1,0:T(8,128)S(1)} %bitcast.25, f32[4,288,128]{2,1,0:T(8,128)S(1)} %get-tuple-element.13.act_ref, bf16[36,64,64]{2,1,0:T(8,128)(2,1)S(1)} %bitcast.23, f32[1,64]{1,0:T(1,128)S(1)} %copy-done.6), custom_call_target="tpu_custom_call" | custom-call | flops 226492416 | bytes 1495296 | tf_op jit(solution)/shard_map/backward/pallas_call | solution.py:226
  10.5 1.0 gradient.1
  11.6 18.1 %all_to_all.46.in_ref = f32[8,152,128]{2,1,0:T(8,128)S(1)} all-to-all(f32[8,152,128]{2,1,0:T(8,128)S(1)} %bitcast.17), channel_id=1, replica_groups=mesh['layer'=64,'dp'=8] {'dp'}, dimensions={0} | all-to-all | bytes 1245184 | tf_op jit(solution)/shard_map/all_to_all | solution.py:276
  29.7 33.7 %all_to_all.47 = f32[64,1,640]{2,1,0:T(1,128)S(1)} all-to-all(f32[64,1,640]{2,1,0:T(1,128)S(1)} %bitcast.24), channel_id=1, replica_groups=mesh['layer'=64,'dp'=8] {'layer'}, dimensions={0} | all-to-all | bytes 327680 | tf_op jit(solution)/shard_map/all_to_all | solution.py:238
  63.4 4.6 %all-to-all-start.2 = ((f32[64,1,640]{2,1,0:T(1,128)}), f32[64,1,640]{2,1,0:T(1,128)S(1)}, u32[]{:S(2)}, u32[]{:S(2)}) async-start(f32[64,1,640]{2,1,0:T(1,128)} %bitcast.8), calls=%async_computation.2 | async-start | bytes 327680 | tf_op jit(solution)/shard_map/all_to_all | solution.py:238
  68.1 0.9 total.1
  68.9 17.2 %all-to-all-done.2 = f32[64,1,640]{2,1,0:T(1,128)S(1)} async-done(((f32[64,1,640]{2,1,0:T(1,128)}), f32[64,1,640]{2,1,0:T(1,128)S(1)}, u32[]{:S(2)}, u32[]{:S(2)}) %all-to-all-start.2) | async-done | bytes 163872 | tf_op jit(solution)/shard_map/all_to_all | solution.py:238
  86.1 4.9 %all-to-all-start.5 = ((f32[8,152,128]{2,1,0:T(8,128)}), f32[8,152,128]{2,1,0:T(8,128)S(1)}, u32[]{:S(2)}, u32[]{:S(2)}) async-start(f32[8,152,128]{2,1,0:T(8,128)} %total.1), calls=%async_computation.5 | async-start | bytes 1245184 | tf_op jit(solution)/shard_map/all_to_all | solution.py:284
  91.0 0.9 scan.1
  91.9 9.1 %all-to-all-done.5 = f32[8,152,128]{2,1,0:T(8,128)S(1)} async-done(((f32[8,152,128]{2,1,0:T(8,128)}), f32[8,152,128]{2,1,0:T(8,128)S(1)}, u32[]{:S(2)}, u32[]{:S(2)}) %all-to-all-start.5) | async-done | bytes 622624 | tf_op jit(solution)/shard_map/all_to_all | solution.py:284
  101.0 4.6 %all-to-all-start.1 = ((f32[64,1,640]{2,1,0:T(1,128)}), f32[64,1,640]{2,1,0:T(1,128)S(1)}, u32[]{:S(2)}, u32[]{:S(2)}) async-start(f32[64,1,640]{2,1,0:T(1,128)} %bitcast.4), calls=%async_computation.1 | async-start | bytes 327680 | tf_op jit(solution)/shard_map/all_to_all | solution.py:238
  105.6 0.9 scan_adj.1
  106.5 18.2 %all-to-all-done.1 = f32[64,1,640]{2,1,0:T(1,128)S(1)} async-done(((f32[64,1,640]{2,1,0:T(1,128)}), f32[64,1,640]{2,1,0:T(1,128)S(1)}, u32[]{:S(2)}, u32[]{:S(2)}) %all-to-all-start.1) | async-done | bytes 163872 | tf_op jit(solution)/shard_map/all_to_all | solution.py:238
  124.7 4.6 %all-to-all-start.3 = ((f32[64,1,640]{2,1,0:T(1,128)}), f32[64,1,640]{2,1,0:T(1,128)S(1)}, u32[]{:S(2)}, u32[]{:S(2)}) async-start(f32[64,1,640]{2,1,0:T(1,128)} %bitcast.10), calls=%async_computation.3 | async-start | bytes 327680 | tf_op jit(solution)/shard_map/all_to_all | solution.py:238
  129.3 1.2 spread.1
  130.5 0.0 copy-done.4
  130.5 0.7 finish.1
  131.3 15.9 %all-to-all-done.3 = f32[64,1,640]{2,1,0:T(1,128)S(1)} async-done(((f32[64,1,640]{2,1,0:T(1,128)}), f32[64,1,640]{2,1,0:T(1,128)S(1)}, u32[]{:S(2)}, u32[]{:S(2)}) %all-to-all-start.3) | async-done | bytes 163872 | tf_op jit(solution)/shard_map/all_to_all | solution.py:238
  147.1 0.7 finish_adj.1
  (3 shorter events, 0.0 us)
Async XLA Ops:
  0.6 1.1 copy-start
  1.7 0.9 copy-start.3
  2.6 0.7 copy-start.5
  3.3 0.7 copy-start.7
  5.7 1.1 copy-start.1
  6.8 0.9 copy-start.2
  7.7 0.7 copy-start.6
  63.4 22.7 %all-to-all-start.2 = ((f32[64,1,640]{2,1,0:T(1,128)}), f32[64,1,640]{2,1,0:T(1,128)S(1)}, u32[]{:S(2)}, u32[]{:S(2)}) async-start(f32[64,1,640]{2,1,0:T(1,128)} %bitcast.8), calls=%async_computation.2 | async-start | bytes 327680 | tf_op jit(solution)/shard_map/all_to_all | solution.py:238
  68.9 61.6 %copy-start.4 = (f32[1,1,24,1536]{3,2,1,0:T(8,128)S(1)}, f32[1,1,24,1536]{3,2,1,0:T(8,128)}, u32[]{:S(2)}) copy-start(f32[1,1,24,1536]{3,2,1,0:T(8,128)} %param.5) | copy-start | bytes 442372
  86.1 14.9 %all-to-all-start.5 = ((f32[8,152,128]{2,1,0:T(8,128)}), f32[8,152,128]{2,1,0:T(8,128)S(1)}, u32[]{:S(2)}, u32[]{:S(2)}) async-start(f32[8,152,128]{2,1,0:T(8,128)} %total.1), calls=%async_computation.5 | async-start | bytes 1245184 | tf_op jit(solution)/shard_map/all_to_all | solution.py:284
  101.0 23.7 %all-to-all-start.1 = ((f32[64,1,640]{2,1,0:T(1,128)}), f32[64,1,640]{2,1,0:T(1,128)S(1)}, u32[]{:S(2)}, u32[]{:S(2)}) async-start(f32[64,1,640]{2,1,0:T(1,128)} %bitcast.4), calls=%async_computation.1 | async-start | bytes 327680 | tf_op jit(solution)/shard_map/all_to_all | solution.py:238
  124.7 22.5 %all-to-all-start.3 = ((f32[64,1,640]{2,1,0:T(1,128)}), f32[64,1,640]{2,1,0:T(1,128)S(1)}, u32[]{:S(2)}, u32[]{:S(2)}) async-start(f32[64,1,640]{2,1,0:T(1,128)} %bitcast.10), calls=%async_computation.3 | async-start | bytes 327680 | tf_op jit(solution)/shard_map/all_to_all | solution.py:238

commit v2 on v1

v2 whole, which is shorter than its diff:
```python
import functools

import jax
import jax.numpy as jnp
from jax import lax
from jax.experimental import pallas as pl
from jax.experimental.pallas import tpu as pltpu
from jax.sharding import PartitionSpec as P

STEP = 0.5
BF = jnp.bfloat16
F32 = jnp.float32
VMEM_BYTES = 12 * 1024 * 1024
BLOCK_VMEM = 67_000_000


def low_lanes(rows):
    return lax.broadcasted_iota(jnp.int32, (rows, 128), 1) < 64


def to_tiles(x):
    return jnp.concatenate([x[:, 128 * k : 128 * k + 128] for k in range(x.shape[1] // 128)], axis=0)


def patches(v, rows_img):
    count = v.shape[0]
    turned = pltpu.roll(v, 64, 1)
    edge = jnp.zeros((rows_img, 128), F32)
    mid = jnp.where(
        low_lanes(count + rows_img),
        jnp.concatenate([edge, turned], axis=0),
        jnp.concatenate([turned, edge], axis=0),
    )
    total = count + rows_img
    groups = total // rows_img
    where_y = lax.broadcasted_iota(jnp.int32, (groups, rows_img, 128), 1)
    up = pltpu.roll(mid, 1, 0).reshape(groups, rows_img, 128)
    up = jnp.where(where_y == 0, 0.0, up).reshape(total, 128)
    down = pltpu.roll(mid, total - 1, 0).reshape(groups, rows_img, 128)
    down = jnp.where(where_y == rows_img - 1, 0.0, down).reshape(total, 128)
    parts = []
    for t in (up, mid, down):
        parts.append(t[:count].astype(BF))
        parts.append(t[rows_img:].astype(BF))
    return jnp.concatenate(parts, axis=1)


def forward_weights(k_ref, layer):
    zero = jnp.zeros((64, 64), BF)
    rows = []
    for dy in range(3):
        tap = [k_ref[layer * 9 + dy * 3 + dx] for dx in range(3)]
        rows.append(jnp.concatenate([tap[0], zero], axis=1))
        rows.append(jnp.concatenate([tap[1], tap[0]], axis=1))
        rows.append(jnp.concatenate([tap[2], tap[1]], axis=1))
        rows.append(jnp.concatenate([zero, tap[2]], axis=1))
    return jnp.concatenate(rows, axis=0)


def backward_weights(k_ref, layer):
    zero = jnp.zeros((64, 64), BF)
    first, second = [], []
    for dy in range(3):
        tap = [k_ref[layer * 9 + (2 - dy) * 3 + dx] for dx in range(3)]
        first += [tap[2], tap[1], tap[0], zero]
        second += [zero, tap[2], tap[1], tap[0]]
    return jnp.concatenate(
        [jnp.concatenate(first, axis=1), jnp.concatenate(second, axis=1)], axis=0
    )


def pack(out_ref, value, other, gain):
    for r in range(4):
        out_ref[pl.ds(r, 64, stride=10), :] = value[64 * r : 64 * r + 64]
        out_ref[pl.ds(5 + r, 64, stride=10), :] = other[64 * r : 64 * r + 64]
    low = low_lanes(32)
    rest, rest_other = value[256:288], other[256:288]
    out_ref[pl.ds(4, 64, stride=10), :] = jnp.concatenate(
        [
            jnp.where(low, rest, pltpu.roll(rest_other, 64, 1)),
            jnp.where(low, pltpu.roll(rest, 64, 1), rest_other),
        ],
        axis=0,
    )
    out_ref[pl.ds(9, 64, stride=10), :] = jnp.broadcast_to(gain, (64, 128))


def unpack(ref):
    low = low_lanes(32)
    extra = ref[pl.ds(4, 64, stride=9), :]
    rest = jnp.where(low, extra[:32], pltpu.roll(extra[32:], 64, 1))
    rest_other = jnp.where(low, pltpu.roll(extra[:32], 64, 1), extra[32:])
    value = [ref[pl.ds(r, 64, stride=9), :] for r in range(4)]
    other = [ref[pl.ds(5 + r, 64, stride=9), :] for r in range(4)]
    return jnp.concatenate(value + [rest], axis=0), jnp.concatenate(other + [rest_other], axis=0)


def from_tiles(out_ref, value, rows_img):
    for k in range(value.shape[0] // rows_img):
        out_ref[:, 128 * k : 128 * k + 128] = value[rows_img * k : rows_img * k + rows_img]


def doubled(row):
    return jnp.concatenate([row, row], axis=1)


def block_kernel(
    depth_count,
    blocks,
    st_hbm,
    adj_hbm,
    k_hbm,
    b_hbm,
    g_hbm,
    send_ref,
    patch_hbm,
    sens_hbm,
    bias_ref,
    st_ref,
    adj_ref,
    k_ref,
    b_ref,
    g_ref,
    act_ref,
    patch_ref,
    sens_ref,
    sems,
    patch_sems,
    sens_sems,
):
    pairs = [(k_hbm, k_ref), (st_hbm, st_ref), (b_hbm, b_ref), (adj_hbm, adj_ref), (g_hbm, g_ref)]
    copies = [pltpu.make_async_copy(a, b, sems.at[i]) for i, (a, b) in enumerate(pairs)]
    for copy in copies:
        copy.start()
    saves = []

    def save(ref, hbm, sem, layer):
        saves.append(pltpu.make_async_copy(ref.at[layer], hbm.at[layer], sem.at[layer]))
        saves[-1].start()

    rows_img = st_ref.shape[0]
    place = lax.axis_index("layer")
    for copy in copies[:3]:
        copy.wait()
    start = to_tiles(st_ref[...])
    field = start
    bias = doubled(b_ref[...])
    for layer in range(depth_count):
        cells = patches(field, rows_img)
        patch_ref[layer] = cells
        save(patch_ref, patch_hbm, patch_sems, layer)
        total = jnp.dot(cells, forward_weights(k_ref, layer), preferred_element_type=F32)
        act = jnp.tanh(total + bias[layer : layer + 1])
        act_ref[layer] = act
        field = field + STEP * act
    for copy in copies[3:]:
        copy.wait()
    gain = doubled(g_ref[...])
    lead = jnp.where(place == 0, jnp.zeros_like(gain), gain)
    tail = jnp.where(place == blocks - 1, jnp.zeros_like(gain), gain)
    offset = field - lead * start
    start_adj = to_tiles(adj_ref[...])
    adjoint = start_adj
    sums = [None] * depth_count
    for layer in reversed(range(depth_count)):
        act = act_ref[layer]
        sens = STEP * (1.0 - act * act) * adjoint
        sens_ref[layer] = sens.astype(BF)
        save(sens_ref, sens_hbm, sens_sems, layer)
        total = jnp.sum(sens, axis=0, keepdims=True)
        sums[layer] = total + pltpu.roll(total, 64, 1)
        adjoint = adjoint + lax.dot_general(
            patches(sens, rows_img),
            backward_weights(k_ref, layer),
            (((1,), (1,)), ((), ())),
            preferred_element_type=F32,
        )
    pack(send_ref, offset, adjoint - tail * start_adj, gain)
    bias_ref[...] = jnp.concatenate(sums + [jnp.zeros((8 - depth_count, 128), F32)], axis=0)
    for copy in saves:
        copy.wait()


def half_gradient(pair, patch_ref, sens_ref):
    low = low_lanes(192)
    both = [
        lax.dot_general(
            patch_ref[2 * pair + q],
            sens_ref[2 * pair + q],
            (((0,), (0,)), ((), ())),
            preferred_element_type=F32,
        )
        for q in range(2)
    ]
    tiles = []
    for dy in range(3):
        one = both[0][256 * dy : 256 * dy + 256]
        two = both[1][256 * dy : 256 * dy + 256]
        tiles.append(
            jnp.where(
                low,
                one[:192] + pltpu.roll(one[64:], 64, 1),
                pltpu.roll(two[:192], 64, 1) + two[64:],
            )
        )
    return tiles


def give_kernel(patch_ref, sens_ref, bias_ref, out_ref):
    core = lax.rem(lax.axis_index("dp"), 2)
    for dy, tile in enumerate(half_gradient(1 - core, patch_ref, sens_ref)):
        out_ref[192 * dy : 192 * dy + 192] = tile
    out_ref[576:584] = bias_ref[...]


def keep_kernel(patch_ref, sens_ref, bias_ref, got_ref, out_ref):
    core = lax.rem(lax.axis_index("dp"), 2)
    for dy, tile in enumerate(half_gradient(core, patch_ref, sens_ref)):
        rows = slice(192 * dy, 192 * dy + 192)
        out_ref[rows] = tile + got_ref[rows]
    out_ref[576:584] = bias_ref[...] + got_ref[576:584]


def total_kernel(scale, own_ref, one_ref, two_ref, three_ref, out_ref):
    out_ref[...] = ((own_ref[...] + two_ref[...]) + (one_ref[...] + three_ref[...])) * scale


def spread_kernel(depth_count, own_ref, other_ref, grad_ref, bias_ref):
    core = lax.rem(lax.axis_index("dp"), 2)
    bias_ref[...] = own_ref[576 : 576 + depth_count, :64]
    for pair, ref in ((core, own_ref), (1 - core, other_ref)):
        for tap in range(9):
            tile = ref[64 * tap : 64 * tap + 64]
            grad_ref[18 * pair + tap] = tile[:, :64]
            grad_ref[18 * pair + 9 + tap] = pltpu.roll(tile, 64, 1)[:, :64]


def scan_kernel(blocks, in_ref, out_ref, left_ref, right_ref):
    gains = in_ref[pl.ds(9, blocks, stride=10), :]
    value = jnp.zeros((5, 128), F32)
    other = jnp.zeros((5, 128), F32)
    for step in range(blocks):
        back = blocks - 1 - step
        out_ref[9 * step : 9 * step + 4] = value[:4]
        left_ref[step : step + 1] = value[4:]
        value = gains[step : step + 1] * value + in_ref[10 * step : 10 * step + 5]
        other = gains[back : back + 1] * other + in_ref[10 * back + 4 : 10 * back + 9]
        out_ref[9 * back + 5 : 9 * back + 9] = other[1:]
        right_ref[back : back + 1] = other[:1]
    out_ref[pl.ds(4, blocks, stride=9), :] = jnp.where(
        low_lanes(blocks), left_ref[...], right_ref[...]
    )


def finish_kernel(rows_img, in_ref, st_hbm, out_ref, adj_ref):
    value, other = unpack(in_ref)
    from_tiles(out_ref, value, rows_img)
    from_tiles(adj_ref, other, rows_img)

    @pl.when(lax.axis_index("layer") == 0)
    def _():
        pltpu.sync_copy(st_hbm, out_ref)


def call(kernel, outs, *args, flops=0, anywhere=(), away=(), scratch=(), room=VMEM_BYTES):
    shapes = [jax.ShapeDtypeStruct(s, d) for s, d in outs]
    size = sum(a.size * a.dtype.itemsize for a in list(args) + shapes)
    near = pl.BlockSpec(memory_space=pltpu.VMEM)
    far = pl.BlockSpec(memory_space=pltpu.HBM)
    return pl.pallas_call(
        kernel,
        out_shape=shapes,
        in_specs=[far if i in anywhere else near for i in range(len(args))],
        out_specs=[far if i in away else near for i in range(len(outs))],
        scratch_shapes=list(scratch),
        compiler_params=pltpu.CompilerParams(vmem_limit_bytes=room),
        cost_estimate=pl.CostEstimate(flops=flops, bytes_accessed=size, transcendentals=0),
    )(*args)


def exchange(rows, count):
    moved = lax.all_to_all(rows.reshape(count, -1), "layer", 0, 0, tiled=True)
    return moved.reshape(rows.shape)


def body(states, adjoints, kernels, biases, coarse_gain):
    rows_img, flat = states.shape[2:]
    depth_count = kernels.shape[0]
    blocks, parts = lax.axis_size("layer"), lax.axis_size("dp")
    tiles = rows_img * flat // 128
    state = states.reshape(rows_img, flat)
    adjoint = adjoints.reshape(rows_img, flat)
    taps = kernels.reshape(depth_count * 9, 64, 64)
    image = ((rows_img, flat), F32)
    half = ((584, 128), F32)
    work = tiles * 768 * 256
    swap = [(i, i ^ 1) for i in range(parts)]
    send, cells, sens, bias = call(
        functools.partial(block_kernel, depth_count, blocks),
        [
            ((10 * blocks, 128), F32),
            ((depth_count, tiles, 768), BF),
            ((depth_count, tiles, 128), BF),
            ((8, 128), F32),
        ],
        state, adjoint, taps, biases, coarse_gain,
        flops=2 * depth_count * work,
        anywhere=(0, 1, 2, 3, 4),
        away=(1, 2),
        room=BLOCK_VMEM,
        scratch=(
            pltpu.VMEM(image[0], F32),
            pltpu.VMEM(image[0], F32),
            pltpu.VMEM(taps.shape, BF),
            pltpu.VMEM(biases.shape, F32),
            pltpu.VMEM(coarse_gain.shape, F32),
            pltpu.VMEM((depth_count, tiles, 128), F32),
            pltpu.VMEM((depth_count, tiles, 768), BF),
            pltpu.VMEM((depth_count, tiles, 128), BF),
            pltpu.SemaphoreType.DMA((5,)),
            pltpu.SemaphoreType.DMA((depth_count,)),
            pltpu.SemaphoreType.DMA((depth_count,)),
        ),
    )
    came = exchange(send, blocks)
    (give,) = call(give_kernel, [half], cells, sens, bias, flops=2 * work)
    got = lax.ppermute(give, "dp", swap)
    (mine,) = call(keep_kernel, [half], cells, sens, bias, got, flops=2 * work)
    ring = []
    for hop in range(1, 4):
        path = [(i, (i + 2 * hop) % parts) for i in range(parts)]
        ring.append(lax.ppermute(mine, "dp", path))
    (back,) = call(
        functools.partial(scan_kernel, blocks),
        [((9 * blocks, 128), F32)],
        came,
        scratch=(pltpu.VMEM((blocks, 128), F32), pltpu.VMEM((blocks, 128), F32)),
    )
    home = exchange(back, blocks)
    (mine,) = call(functools.partial(total_kernel, 1.0 / parts), [half], mine, *ring)
    theirs = lax.ppermute(mine, "dp", swap)
    grad, bias_grad = call(
        functools.partial(spread_kernel, depth_count),
        [((depth_count * 9, 64, 64), F32), ((depth_count, 64), F32)],
        mine, theirs,
    )
    states_new, adjoints_new = call(
        functools.partial(finish_kernel, rows_img), [image, image], home, state,
        anywhere=(1,),
    )
    return (
        states_new.reshape(states.shape),
        adjoints_new.reshape(adjoints.shape),
        grad.reshape(kernels.shape),
        bias_grad,
    )


def solution(mesh):
    return jax.shard_map(
        body,
        mesh=mesh,
        in_specs=(
            P("layer", "dp", None, None),
            P("layer", "dp", None, None),
            P("layer", None, None, None, None),
            P("layer", None),
            P("layer", None),
        ),
        out_specs=(
            P("layer", "dp", None, None),
            P("layer", "dp", None, None),
            P("layer", None, None, None, None),
            P("layer", None),
        ),
        check_vma=False,
    )
```

time: 148 us -> 92.5 us (0.62)
  the two profiles are of different devices: /device:TPU:8 before, /device:TPU:1 now
where the time goes in v2:
time: 92.5 us; the launch traced here: 92.1 us
  blocking collectives  41.5 us (45%)
  starting transfers between devices  22.8 us (25%)
  waiting for transfers between devices  16.3 us (18%)
  Pallas kernels  9.66 us (10%)
  local copies, waits for them, and re-layouts  0.97 us (1%)
    all_to_all x1, blocking collectives, exchange(): moved = lax.all_to_all(rows.reshape(count, -1), 'layer', 0, 0, tiled=True)  41.5 us
    ppermute x3, waiting for transfers between devices, body(): ring.append(lax.ppermute(mine, 'dp', path))  13.9 us
    pallas_call x7, Pallas kernels, call(): pl.pallas_call(kernel, out_shape=shapes, in_specs=[far if i in anywhere e...  9.66 us
    ppermute x3, starting transfers between devices, body(): ring.append(lax.ppermute(mine, 'dp', path))  9.49 us
    all_to_all x1, starting transfers between devices, exchange(): moved = lax.all_to_all(rows.reshape(count, -1), 'layer', 0, 0, tiled=True)  7.08 us
    ppermute x1, starting transfers between devices, body(): got = lax.ppermute(give, 'dp', swap)  3.85 us
    ppermute x1, starting transfers between devices, body(): theirs = lax.ppermute(mine, 'dp', swap)  2.4 us
  transfers between devices with their start and end apart: 6, of which 4 were waited for; matrix products, arithmetic and copies ran while one was open for 0% of the time, Pallas kernels for 3%

profile of v2, /device:TPU:1, one launch (start us, length us, event | category | flops | bytes accessed | tf_op | source)
XLA Modules:
  0.0 92.1 jit_solution(4275556676961222686)
XLA Ops:
  0.6 5.4 %shard_map.84 = (f32[640,128]{1,0:T(8,128)}, bf16[4,288,768]{2,1,0:T(8,128)(2,1)}, bf16[4,288,128]{2,1,0:T(8,128)(2,1)}, f32[8,128]{1,0:T(8,128)}) custom-call(f32[24,1536]{1,0:T(8,128)} %bitcast.12, f32[24,1536]{1,0:T(8,128)} %bitcast.17, bf16[36,64,64]{2,1,0:T(8,128)(2,1)} %bitcast.16, f32[4,64]{1,0:T(4,128)} %b_hbm.1, f32[1,64]{1,0:T(1,128)} %g_hbm.1), custom_call_target="tpu_custom_call" | custom-call | flops 452984832 | bytes 2987264 | tf_op jit(solution)/shard_map/pallas_call | solution.py:270
  6.0 0.0 copy-start
  6.0 0.0 copy-start.3
  6.0 41.5 %all_to_all.18 = f32[64,1,1280]{2,1,0:T(1,128)S(1)} all-to-all(f32[64,1,1280]{2,1,0:T(1,128)} %bitcast.14), channel_id=1, replica_groups=mesh['layer'=64,'dp'=8] {'layer'}, dimensions={0} | all-to-all | bytes 655360 | tf_op jit(solution)/shard_map/all_to_all | solution.py:282
  47.6 0.9 shard_map.85
  48.4 7.1 %all-to-all-start.1 = ((f32[64,1,1152]{2,1,0:T(1,128)}), f32[64,1,1152]{2,1,0:T(1,128)S(1)}, u32[]{:S(2)}, u32[]{:S(2)}) async-start(f32[64,1,1152]{2,1,0:T(1,128)} %bitcast.5), calls=%async_computation.1 | async-start | bytes 589824 | tf_op jit(solution)/shard_map/all_to_all | solution.py:282
  55.5 0.0 copy-done
  55.5 0.0 copy-done.3
  55.5 0.0 copy-start.1
  55.5 1.0 %copy-done.1 = bf16[4,288,128]{2,1,0:T(8,128)(2,1)S(1)} copy-done((bf16[4,288,128]{2,1,0:T(8,128)(2,1)S(1)}, bf16[4,288,128]{2,1,0:T(8,128)(2,1)}, u32[]{:S(2)}) %copy-start.1) | copy-done | bytes 294936
  56.5 0.6 shard_map.87
  57.1 0.0 copy-start.2
  57.1 3.9 %collective-permute-start = (f32[584,128]{1,0:T(8,128)S(1)}, f32[584,128]{1,0:T(8,128)S(1)}, u32[]{:S(2)}, u32[]{:S(2)}) collective-permute-start(f32[584,128]{1,0:T(8,128)S(1)} %shard_map.87), channel_id=1, source_target_pairs={{0,1},{1,0},{2,3},{3,2},{4,5},{5,4},{6,7},{7,6},{8,9},{9,8},{10,11... | collective-permute-start | bytes 897032 | tf_op jit(solution)/shard_map/ppermute | solution.py:327
  60.9 1.2 %collective-permute-done.got_ref = f32[584,128]{1,0:T(8,128)S(1)} collective-permute-done((f32[584,128]{1,0:T(8,128)S(1)}, f32[584,128]{1,0:T(8,128)S(1)}, u32[]{:S(2)}, u32[]{:S(2)}) %collective-permute-start) | collective-permute-done | bytes 299040 | tf_op jit(solution)/shard_map/ppermute | solution.py:327
  62.1 0.6 shard_map.88.own_ref
  62.7 4.6 %collective-permute-start.3 = (f32[584,128]{1,0:T(8,128)S(1)}, f32[584,128]{1,0:T(8,128)S(1)}, u32[]{:S(2)}, u32[]{:S(2)}) collective-permute-start(f32[584,128]{1,0:T(8,128)S(1)} %shard_map.88.own_ref), channel_id=1, source_target_pairs={{0,6},{1,7},{2,0},{3,1},{4,2},{5,3},{6,4},{7,5},{8,14},{9,15},{10,... | collective-permute-start | bytes 897032 | tf_op jit(solution)/shard_map/ppermute | solution.py:332
  67.3 2.3 %collective-permute-start.2 = (f32[584,128]{1,0:T(8,128)S(1)}, f32[584,128]{1,0:T(8,128)S(1)}, u32[]{:S(2)}, u32[]{:S(2)}) collective-permute-start(f32[584,128]{1,0:T(8,128)S(1)} %shard_map.88.own_ref), channel_id=1, source_target_pairs={{0,4},{1,5},{2,6},{3,7},{4,0},{5,1},{6,2},{7,3},{8,12},{9,13},{10,... | collective-permute-start | bytes 897032 | tf_op jit(solution)/shard_map/ppermute | solution.py:332
  69.6 2.6 %collective-permute-start.1 = (f32[584,128]{1,0:T(8,128)S(1)}, f32[584,128]{1,0:T(8,128)S(1)}, u32[]{:S(2)}, u32[]{:S(2)}) collective-permute-start(f32[584,128]{1,0:T(8,128)S(1)} %shard_map.88.own_ref), channel_id=1, source_target_pairs={{0,2},{1,3},{2,4},{3,5},{4,6},{5,7},{6,0},{7,1},{8,10},{9,11},{10,... | collective-permute-start | bytes 897032 | tf_op jit(solution)/shard_map/ppermute | solution.py:332
  72.2 7.4 %collective-permute-done.3.three_ref = f32[584,128]{1,0:T(8,128)S(1)} collective-permute-done((f32[584,128]{1,0:T(8,128)S(1)}, f32[584,128]{1,0:T(8,128)S(1)}, u32[]{:S(2)}, u32[]{:S(2)}) %collective-permute-start.3) | collective-permute-done | bytes 299040 | tf_op jit(solution)/shard_map/ppermute | solution.py:332
  79.7 0.0 collective-permute-done.2.two_ref
  79.7 6.5 %collective-permute-done.1.one_ref = f32[584,128]{1,0:T(8,128)S(1)} collective-permute-done((f32[584,128]{1,0:T(8,128)S(1)}, f32[584,128]{1,0:T(8,128)S(1)}, u32[]{:S(2)}, u32[]{:S(2)}) %collective-permute-start.1) | collective-permute-done | bytes 299040 | tf_op jit(solution)/shard_map/ppermute | solution.py:332
  86.2 0.1 shard_map.89.own_ref
  86.3 2.4 %collective-permute-start.4 = (f32[584,128]{1,0:T(8,128)S(1)}, f32[584,128]{1,0:T(8,128)S(1)}, u32[]{:S(2)}, u32[]{:S(2)}) collective-permute-start(f32[584,128]{1,0:T(8,128)S(1)} %shard_map.89.own_ref), channel_id=1, source_target_pairs={{0,1},{1,0},{2,3},{3,2},{4,5},{5,4},{6,7},{7,6},{8,9},{9,8},{10,11... | collective-permute-start | bytes 897032 | tf_op jit(solution)/shard_map/ppermute | solution.py:341
  88.7 1.2 %collective-permute-done.4.other_ref = f32[584,128]{1,0:T(8,128)S(1)} collective-permute-done((f32[584,128]{1,0:T(8,128)S(1)}, f32[584,128]{1,0:T(8,128)S(1)}, u32[]{:S(2)}, u32[]{:S(2)}) %collective-permute-start.4) | collective-permute-done | bytes 299040 | tf_op jit(solution)/shard_map/ppermute | solution.py:341
  89.9 1.3 %shard_map.90 = (f32[36,64,64]{2,1,0:T(8,128)}, f32[4,64]{1,0:T(4,128)}) custom-call(f32[584,128]{1,0:T(8,128)S(1)} %shard_map.89.own_ref, f32[584,128]{1,0:T(8,128)S(1)} %collective-permute-done.4.other_ref), custom_call_target="tpu_custom_call" | custom-call | bytes 1188864 | tf_op jit(solution)/shard_map/pallas_call | solution.py:270
  91.1 0.0 all-to-all-done.1
  91.1 0.0 copy-done.2
  91.1 1.0 %shard_map.86 = (f32[24,1536]{1,0:T(8,128)}, f32[24,1536]{1,0:T(8,128)}) custom-call(f32[576,128]{1,0:T(8,128)S(1)} %bitcast.11, f32[24,1536]{1,0:T(8,128)S(1)} %bitcast.13), custom_call_target="tpu_custom_call" | custom-call | bytes 737280 | tf_op jit(solution)/shard_map/pallas_call | solution.py:270
Async XLA Ops:
  6.0 49.5 %copy-start = (bf16[4,288,768]{2,1,0:T(8,128)(2,1)S(1)}, bf16[4,288,768]{2,1,0:T(8,128)(2,1)}, u32[]{:S(2)}) copy-start(bf16[4,288,768]{2,1,0:T(8,128)(2,1)} %get-tuple-element.15.patch_ref) | copy-start | bytes 5308420
  6.0 49.5 %copy-start.3 = (f32[8,128]{1,0:T(8,128)S(1)}, f32[8,128]{1,0:T(8,128)}, u32[]{:S(2)}) copy-start(f32[8,128]{1,0:T(8,128)} %get-tuple-element.17.bias_ref) | copy-start | bytes 12292
  48.4 42.7 %all-to-all-start.1 = ((f32[64,1,1152]{2,1,0:T(1,128)}), f32[64,1,1152]{2,1,0:T(1,128)S(1)}, u32[]{:S(2)}, u32[]{:S(2)}) async-start(f32[64,1,1152]{2,1,0:T(1,128)} %bitcast.5), calls=%async_computation.1 | async-start | bytes 589824 | tf_op jit(solution)/shard_map/all_to_all | solution.py:282
  55.5 1.0 %copy-start.1 = (bf16[4,288,128]{2,1,0:T(8,128)(2,1)S(1)}, bf16[4,288,128]{2,1,0:T(8,128)(2,1)}, u32[]{:S(2)}) copy-start(bf16[4,288,128]{2,1,0:T(8,128)(2,1)} %get-tuple-element.16.sens_ref) | copy-start | bytes 884740
  57.1 34.1 %copy-start.2 = (f32[1,1,24,1536]{3,2,1,0:T(8,128)S(1)}, f32[1,1,24,1536]{3,2,1,0:T(8,128)}, u32[]{:S(2)}) copy-start(f32[1,1,24,1536]{3,2,1,0:T(8,128)} %param.5) | copy-start | bytes 442372
  57.1 5.1 %collective-permute-start = (f32[584,128]{1,0:T(8,128)S(1)}, f32[584,128]{1,0:T(8,128)S(1)}, u32[]{:S(2)}, u32[]{:S(2)}) collective-permute-start(f32[584,128]{1,0:T(8,128)S(1)} %shard_map.87), channel_id=1, source_target_pairs={{0,1},{1,0},{2,3},{3,2},{4,5},{5,4},{6,7},{7,6},{8,9},{9,8},{10,11... | collective-permute-start | bytes 897032 | tf_op jit(solution)/shard_map/ppermute | solution.py:327
  62.7 17.0 %collective-permute-start.3 = (f32[584,128]{1,0:T(8,128)S(1)}, f32[584,128]{1,0:T(8,128)S(1)}, u32[]{:S(2)}, u32[]{:S(2)}) collective-permute-start(f32[584,128]{1,0:T(8,128)S(1)} %shard_map.88.own_ref), channel_id=1, source_target_pairs={{0,6},{1,7},{2,0},{3,1},{4,2},{5,3},{6,4},{7,5},{8,14},{9,15},{10,... | collective-permute-start | bytes 897032 | tf_op jit(solution)/shard_map/ppermute | solution.py:332
  67.3 12.3 %collective-permute-start.2 = (f32[584,128]{1,0:T(8,128)S(1)}, f32[584,128]{1,0:T(8,128)S(1)}, u32[]{:S(2)}, u32[]{:S(2)}) collective-permute-start(f32[584,128]{1,0:T(8,128)S(1)} %shard_map.88.own_ref), channel_id=1, source_target_pairs={{0,4},{1,5},{2,6},{3,7},{4,0},{5,1},{6,2},{7,3},{8,12},{9,13},{10,... | collective-permute-start | bytes 897032 | tf_op jit(solution)/shard_map/ppermute | solution.py:332
  69.6 16.5 %collective-permute-start.1 = (f32[584,128]{1,0:T(8,128)S(1)}, f32[584,128]{1,0:T(8,128)S(1)}, u32[]{:S(2)}, u32[]{:S(2)}) collective-permute-start(f32[584,128]{1,0:T(8,128)S(1)} %shard_map.88.own_ref), channel_id=1, source_target_pairs={{0,2},{1,3},{2,4},{3,5},{4,6},{5,7},{6,0},{7,1},{8,10},{9,11},{10,... | collective-permute-start | bytes 897032 | tf_op jit(solution)/shard_map/ppermute | solution.py:332
  86.3 3.6 %collective-permute-start.4 = (f32[584,128]{1,0:T(8,128)S(1)}, f32[584,128]{1,0:T(8,128)S(1)}, u32[]{:S(2)}, u32[]{:S(2)}) collective-permute-start(f32[584,128]{1,0:T(8,128)S(1)} %shard_map.89.own_ref), channel_id=1, source_target_pairs={{0,1},{1,0},{2,3},{3,2},{4,5},{5,4},{6,7},{7,6},{8,9},{9,8},{10,11... | collective-permute-start | bytes 897032 | tf_op jit(solution)/shard_map/ppermute | solution.py:341

commit v3 on v2

--- a/solution.py
+++ b/solution.py
@@ -12,6 +12,8 @@
 F32 = jnp.float32
 VMEM_BYTES = 12 * 1024 * 1024
 BLOCK_VMEM = 67_000_000
+ROW = 4
+QUARTER = 72
 
 
 def low_lanes(rows):
@@ -69,29 +71,30 @@
     )
 
 
-def pack(out_ref, value, other, gain):
+def pack(out_ref, count, value, other, gain):
     for r in range(4):
-        out_ref[pl.ds(r, 64, stride=10), :] = value[64 * r : 64 * r + 64]
-        out_ref[pl.ds(5 + r, 64, stride=10), :] = other[64 * r : 64 * r + 64]
-    low = low_lanes(32)
-    rest, rest_other = value[256:288], other[256:288]
-    out_ref[pl.ds(4, 64, stride=10), :] = jnp.concatenate(
+        out_ref[pl.ds(r, count, stride=10), :] = value[count * r : count * r + count]
+        out_ref[pl.ds(5 + r, count, stride=10), :] = other[count * r : count * r + count]
+    low = low_lanes(count // 2)
+    rest, rest_other = value[4 * count :], other[4 * count :]
+    out_ref[pl.ds(4, count, stride=10), :] = jnp.concatenate(
         [
             jnp.where(low, rest, pltpu.roll(rest_other, 64, 1)),
             jnp.where(low, pltpu.roll(rest, 64, 1), rest_other),
         ],
         axis=0,
     )
-    out_ref[pl.ds(9, 64, stride=10), :] = jnp.broadcast_to(gain, (64, 128))
-
-
-def unpack(ref):
-    low = low_lanes(32)
-    extra = ref[pl.ds(4, 64, stride=9), :]
-    rest = jnp.where(low, extra[:32], pltpu.roll(extra[32:], 64, 1))
-    rest_other = jnp.where(low, pltpu.roll(extra[:32], 64, 1), extra[32:])
-    value = [ref[pl.ds(r, 64, stride=9), :] for r in range(4)]
-    other = [ref[pl.ds(5 + r, 64, stride=9), :] for r in range(4)]
+    out_ref[pl.ds(9, count, stride=10), :] = jnp.broadcast_to(gain, (count, 128))
+
+
+def unpack(ref, count):
+    low = low_lanes(count // 2)
+    extra = ref[pl.ds(4, count, stride=9), :]
+    top, bottom = extra[: count // 2], extra[count // 2 :]
+    rest = jnp.where(low, top, pltpu.roll(bottom, 64, 1))
+    rest_other = jnp.where(low, pltpu.roll(top, 64, 1), bottom)
+    value = [ref[pl.ds(r, count, stride=9), :] for r in range(4)]
+    other = [ref[pl.ds(5 + r, count, stride=9), :] for r in range(4)]
     return jnp.concatenate(value + [rest], axis=0), jnp.concatenate(other + [rest_other], axis=0)
 
 
@@ -102,6 +105,23 @@
 
 def doubled(row):
     return jnp.concatenate([row, row], axis=1)
+
+
+def half_gradient(out_ref, cells, senses, bias_rows):
+    low = low_lanes(192)
+    one, two = [
+        lax.dot_general(c, s, (((0,), (0,)), ((), ())), preferred_element_type=F32)
+        for c, s in zip(cells, senses)
+    ]
+    for dy in range(3):
+        first = one[256 * dy : 256 * dy + 256]
+        second = two[256 * dy : 256 * dy + 256]
+        out_ref[192 * dy : 192 * dy + 192] = jnp.where(
+            low,
+            first[:192] + pltpu.roll(first[64:], 64, 1),
+            pltpu.roll(second[:192], 64, 1) + second[64:],
+        )
+    out_ref[576:584] = bias_rows
 
 
 def block_kernel(
@@ -113,9 +133,8 @@
     b_hbm,
     g_hbm,
     send_ref,
-    patch_hbm,
-    sens_hbm,
-    bias_ref,
+    give_ref,
+    keep_ref,
     st_ref,
     adj_ref,
     k_ref,
@@ -125,21 +144,14 @@
     patch_ref,
     sens_ref,
     sems,
-    patch_sems,
-    sens_sems,
 ):
     pairs = [(k_hbm, k_ref), (st_hbm, st_ref), (b_hbm, b_ref), (adj_hbm, adj_ref), (g_hbm, g_ref)]
     copies = [pltpu.make_async_copy(a, b, sems.at[i]) for i, (a, b) in enumerate(pairs)]
     for copy in copies:
         copy.start()
-    saves = []
-
-    def save(ref, hbm, sem, layer):
-        saves.append(pltpu.make_async_copy(ref.at[layer], hbm.at[layer], sem.at[layer]))
-        saves[-1].start()
-
     rows_img = st_ref.shape[0]
     place = lax.axis_index("layer")
+    core = lax.rem(lax.axis_index("dp"), 2)
     for copy in copies[:3]:
         copy.wait()
     start = to_tiles(st_ref[...])
@@ -148,7 +160,6 @@
     for layer in range(depth_count):
         cells = patches(field, rows_img)
         patch_ref[layer] = cells
-        save(patch_ref, patch_hbm, patch_sems, layer)
         total = jnp.dot(cells, forward_weights(k_ref, layer), preferred_element_type=F32)
         act = jnp.tanh(total + bias[layer : layer + 1])
         act_ref[layer] = act
@@ -166,7 +177,6 @@
         act = act_ref[layer]
         sens = STEP * (1.0 - act * act) * adjoint
         sens_ref[layer] = sens.astype(BF)
-        save(sens_ref, sens_hbm, sens_sems, layer)
         total = jnp.sum(sens, axis=0, keepdims=True)
         sums[layer] = total + pltpu.roll(total, 64, 1)
         adjoint = adjoint + lax.dot_general(
@@ -175,50 +185,24 @@
             (((1,), (1,)), ((), ())),
             preferred_element_type=F32,
         )
-    pack(send_ref, offset, adjoint - tail * start_adj, gain)
-    bias_ref[...] = jnp.concatenate(sums + [jnp.zeros((8 - depth_count, 128), F32)], axis=0)
-    for copy in saves:
-        copy.wait()
-
-
-def half_gradient(pair, patch_ref, sens_ref):
-    low = low_lanes(192)
-    both = [
-        lax.dot_general(
-            patch_ref[2 * pair + q],
-            sens_ref[2 * pair + q],
-            (((0,), (0,)), ((), ())),
-            preferred_element_type=F32,
+    back = adjoint - tail * start_adj
+    for part in range(ROW):
+        rows = slice(QUARTER * part, QUARTER * part + QUARTER)
+        send_ref[part, :QUARTER] = offset[rows]
+        send_ref[part, QUARTER : 2 * QUARTER] = back[rows]
+        send_ref[part, 2 * QUARTER :] = jnp.broadcast_to(gain, (8, 128))
+    bias_rows = jnp.concatenate(sums + [jnp.zeros((8 - depth_count, 128), F32)], axis=0)
+    for pair, ref in ((1 - core, give_ref), (core, keep_ref)):
+        half_gradient(
+            ref,
+            [patch_ref[2 * pair + q] for q in range(2)],
+            [sens_ref[2 * pair + q] for q in range(2)],
+            bias_rows,
         )
-        for q in range(2)
-    ]
-    tiles = []
-    for dy in range(3):
-        one = both[0][256 * dy : 256 * dy + 256]
-        two = both[1][256 * dy : 256 * dy + 256]
-        tiles.append(
-            jnp.where(
-                low,
-                one[:192] + pltpu.roll(one[64:], 64, 1),
-                pltpu.roll(two[:192], 64, 1) + two[64:],
-            )
-        )
-    return tiles
-
-
-def give_kernel(patch_ref, sens_ref, bias_ref, out_ref):
-    core = lax.rem(lax.axis_index("dp"), 2)
-    for dy, tile in enumerate(half_gradient(1 - core, patch_ref, sens_ref)):
-        out_ref[192 * dy : 192 * dy + 192] = tile
-    out_ref[576:584] = bias_ref[...]
-
-
-def keep_kernel(patch_ref, sens_ref, bias_ref, got_ref, out_ref):
-    core = lax.rem(lax.axis_index("dp"), 2)
-    for dy, tile in enumerate(half_gradient(core, patch_ref, sens_ref)):
-        rows = slice(192 * dy, 192 * dy + 192)
-        out_ref[rows] = tile + got_ref[rows]
-    out_ref[576:584] = bias_ref[...] + got_ref[576:584]
+
+
+def keep_kernel(keep_ref, got_ref, out_ref):
+    out_ref[...] = keep_ref[...] + got_ref[...]
 
 
 def total_kernel(scale, own_ref, one_ref, two_ref, three_ref, out_ref):
@@ -235,25 +219,57 @@
             grad_ref[18 * pair + 9 + tap] = pltpu.roll(tile, 64, 1)[:, :64]
 
 
-def scan_kernel(blocks, in_ref, out_ref, left_ref, right_ref):
-    gains = in_ref[pl.ds(9, blocks, stride=10), :]
+def row_parts(ref, part):
+    return (
+        ref[part, :QUARTER],
+        ref[part, QUARTER : 2 * QUARTER],
+        ref[part, 2 * QUARTER : 2 * QUARTER + 1],
+    )
+
+
+def compose_kernel(count, in_ref, out_ref):
+    parts = [row_parts(in_ref, part) for part in range(ROW)]
+    value, other, gain = parts[0][0], parts[-1][1], parts[0][2]
+    for ahead, _, factor in parts[1:]:
+        value = factor * value + ahead
+        gain = gain * factor
+    for _, behind, factor in reversed(parts[:-1]):
+        other = factor * other + behind
+    pack(out_ref, count, value, other, gain)
+
+
+def scan_kernel(count, in_ref, out_ref, left_ref, right_ref):
+    gains = in_ref[pl.ds(9, count, stride=10), :]
     value = jnp.zeros((5, 128), F32)
     other = jnp.zeros((5, 128), F32)
-    for step in range(blocks):
-        back = blocks - 1 - step
+    for step in range(count):
+        back = count - 1 - step
         out_ref[9 * step : 9 * step + 4] = value[:4]
         left_ref[step : step + 1] = value[4:]
+        out_ref[9 * back + 5 : 9 * back + 9] = other[1:]
+        right_ref[back : back + 1] = other[:1]
         value = gains[step : step + 1] * value + in_ref[10 * step : 10 * step + 5]
         other = gains[back : back + 1] * other + in_ref[10 * back + 4 : 10 * back + 9]
-        out_ref[9 * back + 5 : 9 * back + 9] = other[1:]
-        right_ref[back : back + 1] = other[:1]
-    out_ref[pl.ds(4, blocks, stride=9), :] = jnp.where(
-        low_lanes(blocks), left_ref[...], right_ref[...]
-    )
+    out_ref[pl.ds(4, count, stride=9), :] = jnp.where(
+        low_lanes(count), left_ref[...], right_ref[...]
+    )
+
+
+def expand_kernel(count, home_ref, came_ref, out_ref):
+    value, other = unpack(home_ref, count)
+    for part in range(ROW):
+        back = ROW - 1 - part
+        ahead, _, gain = row_parts(came_ref, part)
+        out_ref[part, :QUARTER] = value
+        value = gain * value + ahead
+        _, behind, gain = row_parts(came_ref, back)
+        other = gain * other + behind
+        out_ref[back, QUARTER:] = other
 
 
 def finish_kernel(rows_img, in_ref, st_hbm, out_ref, adj_ref):
-    value, other = unpack(in_ref)
+    value = jnp.concatenate([in_ref[part, :QUARTER] for part in range(ROW)], axis=0)
+    other = jnp.concatenate([in_ref[part, QUARTER:] for part in range(ROW)], axis=0)
     from_tiles(out_ref, value, rows_img)
     from_tiles(adj_ref, other, rows_img)
 
@@ -278,9 +294,17 @@
     )(*args)
 
 
-def exchange(rows, count):
-    moved = lax.all_to_all(rows.reshape(count, -1), "layer", 0, 0, tiled=True)
-    return moved.reshape(rows.shape)
+def exchange(array, groups):
+    count = len(groups[0])
+    moved = lax.all_to_all(
+        array.reshape(count, -1, 128) if array.ndim == 3 else array.reshape(count, -1),
+        "layer",
+        0,
+        0,
+        axis_index_groups=groups,
+        tiled=True,
+    )
+    return moved.reshape(array.shape)
 
 
 def body(states, adjoints, kernels, biases, coarse_gain):
@@ -288,25 +312,21 @@
     depth_count = kernels.shape[0]
     blocks, parts = lax.axis_size("layer"), lax.axis_size("dp")
     tiles = rows_img * flat // 128
+    count = blocks // ROW
+    rows = [[z * ROW + x for x in range(ROW)] for z in range(count)]
+    columns = [[z * ROW + x for z in range(count)] for x in range(ROW)]
     state = states.reshape(rows_img, flat)
     adjoint = adjoints.reshape(rows_img, flat)
     taps = kernels.reshape(depth_count * 9, 64, 64)
     image = ((rows_img, flat), F32)
     half = ((584, 128), F32)
-    work = tiles * 768 * 256
     swap = [(i, i ^ 1) for i in range(parts)]
-    send, cells, sens, bias = call(
+    send, give, keep = call(
         functools.partial(block_kernel, depth_count, blocks),
-        [
-            ((10 * blocks, 128), F32),
-            ((depth_count, tiles, 768), BF),
-            ((depth_count, tiles, 128), BF),
-            ((8, 128), F32),
-        ],
+        [((ROW, 2 * QUARTER + 8, 128), F32), half, half],
         state, adjoint, taps, biases, coarse_gain,
-        flops=2 * depth_count * work,
+        flops=3 * depth_count * tiles * 768 * 256,
         anywhere=(0, 1, 2, 3, 4),
-        away=(1, 2),
         room=BLOCK_VMEM,
         scratch=(
             pltpu.VMEM(image[0], F32),
@@ -318,34 +338,39 @@
             pltpu.VMEM((depth_count, tiles, 768), BF),
             pltpu.VMEM((depth_count, tiles, 128), BF),
             pltpu.SemaphoreType.DMA((5,)),
-            pltpu.SemaphoreType.DMA((depth_count,)),
-            pltpu.SemaphoreType.DMA((depth_count,)),
         ),
     )
-    came = exchange(send, blocks)
-    (give,) = call(give_kernel, [half], cells, sens, bias, flops=2 * work)
+    came = exchange(send, rows)
     got = lax.ppermute(give, "dp", swap)
-    (mine,) = call(keep_kernel, [half], cells, sens, bias, got, flops=2 * work)
+    (mine,) = call(keep_kernel, [half], keep, got)
+    (totals,) = call(functools.partial(compose_kernel, count), [((10 * count, 128), F32)], came)
+    column = exchange(totals, columns)
     ring = []
     for hop in range(1, 4):
         path = [(i, (i + 2 * hop) % parts) for i in range(parts)]
         ring.append(lax.ppermute(mine, "dp", path))
-    (back,) = call(
-        functools.partial(scan_kernel, blocks),
-        [((9 * blocks, 128), F32)],
-        came,
-        scratch=(pltpu.VMEM((blocks, 128), F32), pltpu.VMEM((blocks, 128), F32)),
-    )
-    home = exchange(back, blocks)
+    (before,) = call(
+        functools.partial(scan_kernel, count),
+        [((9 * count, 128), F32)],
+        column,
+        scratch=(pltpu.VMEM((count, 128), F32), pltpu.VMEM((count, 128), F32)),
+    )
+    home = exchange(before, columns)
     (mine,) = call(functools.partial(total_kernel, 1.0 / parts), [half], mine, *ring)
     theirs = lax.ppermute(mine, "dp", swap)
+    (spread,) = call(
+        functools.partial(expand_kernel, count),
+        [((ROW, 2 * QUARTER, 128), F32)],
+        home, came,
+    )
+    result = exchange(spread, rows)
     grad, bias_grad = call(
         functools.partial(spread_kernel, depth_count),
         [((depth_count * 9, 64, 64), F32), ((depth_count, 64), F32)],
         mine, theirs,
     )
     states_new, adjoints_new = call(
-        functools.partial(finish_kernel, rows_img), [image, image], home, state,
+        functools.partial(finish_kernel, rows_img), [image, image], result, state,
         anywhere=(1,),
     )
     return (

time: 92.5 us -> 82.8 us (0.90)
  the two profiles are of different devices: /device:TPU:1 before, /device:TPU:8 now
where the time goes in v3:
time: 82.8 us; the launch traced here: 82.2 us
  starting transfers between devices  47.4 us (57%)
  waiting for transfers between devices  23.9 us (29%)
  Pallas kernels  10.2 us (12%)
    all_to_all x4, starting transfers between devices, exchange(): lax.all_to_all(array.reshape(count, -1, 128) if array.ndim == 3 else arra...  32.8 us
    all_to_all x4, waiting for transfers between devices, exchange(): lax.all_to_all(array.reshape(count, -1, 128) if array.ndim == 3 else arra...  23.8 us
    ppermute x3, starting transfers between devices, body(): ring.append(lax.ppermute(mine, 'dp', path))  10.6 us
    pallas_call x8, Pallas kernels, call(): pl.pallas_call(kernel, out_shape=shapes, in_specs=[far if i in anywhere e...  10.2 us
    ppermute x1, starting transfers between devices, body(): theirs = lax.ppermute(mine, 'dp', swap)  2.05 us
    ppermute x1, starting transfers between devices, body(): got = lax.ppermute(give, 'dp', swap)  1.91 us
  transfers between devices with their start and end apart: 9, of which 4 were waited for; matrix products, arithmetic and copies ran while one was open for 0% of the time, Pallas kernels for 4%

profile of v3, /device:TPU:8, one launch (start us, length us, event | category | flops | bytes accessed | tf_op | source)
XLA Modules:
  0.0 82.2 jit_solution(8262304744735409734)
XLA Ops:
  0.6 5.7 %shard_map.84 = (f32[4,152,128]{2,1,0:T(8,128)}, f32[584,128]{1,0:T(8,128)}, f32[584,128]{1,0:T(8,128)}) custom-call(f32[24,1536]{1,0:T(8,128)} %bitcast.12, f32[24,1536]{1,0:T(8,128)} %bitcast.16, bf16[36,64,64]{2,1,0:T(8,128)(2,1)} %bitcast.15, f32[4,64]{1,0:T(4,128)} %b_hbm.1, f32[1,64]{1,0:T(1,128)} %g_hbm.1), custom_call_target="tpu_custom_call" | custom-call | flops 679477248 | bytes 1500416 | tf_op jit(solution)/shard_map/pallas_call | solution.py:286
  6.4 0.0 copy-start
  6.4 4.4 %all-to-all-start = ((f32[4,152,128]{2,1,0:T(8,128)}), f32[4,152,128]{2,1,0:T(8,128)S(1)}, u32[]{:S(2)}, u32[]{:S(2)}) async-start(f32[4,152,128]{2,1,0:T(8,128)} %get-tuple-element.11), calls=%async_computation | async-start | bytes 622592 | tf_op jit(solution)/shard_map/all_to_all | solution.py:299
  10.8 1.9 %collective-permute-start = (f32[584,128]{1,0:T(8,128)}, f32[584,128]{1,0:T(8,128)S(1)}, u32[]{:S(2)}, u32[]{:S(2)}) collective-permute-start(f32[584,128]{1,0:T(8,128)} %get-tuple-element.15), channel_id=1, source_target_pairs={{0,1},{1,0},{2,3},{3,2},{4,5},{5,4},{6,7},{7,6},{8,9},{9,8},{10,11... | collective-permute-start | bytes 897032 | tf_op jit(solution)/shard_map/ppermute | solution.py:344
  12.7 5.3 %all-to-all-done.in_ref.came_ref = f32[4,152,128]{2,1,0:T(8,128)S(1)} async-done(((f32[4,152,128]{2,1,0:T(8,128)}), f32[4,152,128]{2,1,0:T(8,128)S(1)}, u32[]{:S(2)}, u32[]{:S(2)}) %all-to-all-start) | async-done | bytes 311328 | tf_op jit(solution)/shard_map/all_to_all | solution.py:299
  18.0 0.7 shard_map.85
  18.7 15.2 %all-to-all-start.1 = ((f32[16,1,1280]{2,1,0:T(1,128)}), f32[16,1,1280]{2,1,0:T(1,128)S(1)}, u32[]{:S(2)}, u32[]{:S(2)}) async-start(f32[16,1,1280]{2,1,0:T(1,128)} %bitcast.3), calls=%async_computation.1 | async-start | bytes 163840 | tf_op jit(solution)/shard_map/all_to_all | solution.py:299
  33.9 0.0 collective-permute-done.got_ref
  33.9 0.0 copy-done
  34.0 2.4 %collective-permute-start.3 = (f32[584,128]{1,0:T(8,128)S(1)}, f32[584,128]{1,0:T(8,128)S(1)}, u32[]{:S(2)}, u32[]{:S(2)}) collective-permute-start(f32[584,128]{1,0:T(8,128)S(1)} %shard_map.89.own_ref), channel_id=1, source_target_pairs={{0,6},{1,7},{2,0},{3,1},{4,2},{5,3},{6,4},{7,5},{8,14},{9,15},{10,... | collective-permute-start | bytes 897032 | tf_op jit(solution)/shard_map/ppermute | solution.py:351
  36.4 4.5 %collective-permute-start.2 = (f32[584,128]{1,0:T(8,128)S(1)}, f32[584,128]{1,0:T(8,128)S(1)}, u32[]{:S(2)}, u32[]{:S(2)}) collective-permute-start(f32[584,128]{1,0:T(8,128)S(1)} %shard_map.89.own_ref), channel_id=1, source_target_pairs={{0,4},{1,5},{2,6},{3,7},{4,0},{5,1},{6,2},{7,3},{8,12},{9,13},{10,... | collective-permute-start | bytes 897032 | tf_op jit(solution)/shard_map/ppermute | solution.py:351
  40.9 3.8 %collective-permute-start.1 = (f32[584,128]{1,0:T(8,128)S(1)}, f32[584,128]{1,0:T(8,128)S(1)}, u32[]{:S(2)}, u32[]{:S(2)}) collective-permute-start(f32[584,128]{1,0:T(8,128)S(1)} %shard_map.89.own_ref), channel_id=1, source_target_pairs={{0,2},{1,3},{2,4},{3,5},{4,6},{5,7},{6,0},{7,1},{8,10},{9,11},{10,... | collective-permute-start | bytes 897032 | tf_op jit(solution)/shard_map/ppermute | solution.py:351
  44.7 2.3 %all-to-all-done.1 = f32[16,1,1280]{2,1,0:T(1,128)S(1)} async-done(((f32[16,1,1280]{2,1,0:T(1,128)}), f32[16,1,1280]{2,1,0:T(1,128)S(1)}, u32[]{:S(2)}, u32[]{:S(2)}) %all-to-all-start.1) | async-done | bytes 81952 | tf_op jit(solution)/shard_map/all_to_all | solution.py:299
  47.0 0.7 shard_map.86
  47.7 9.7 %all-to-all-start.2 = ((f32[16,1,1152]{2,1,0:T(1,128)}), f32[16,1,1152]{2,1,0:T(1,128)S(1)}, u32[]{:S(2)}, u32[]{:S(2)}) async-start(f32[16,1,1152]{2,1,0:T(1,128)} %bitcast.5), calls=%async_computation.2 | async-start | bytes 147456 | tf_op jit(solution)/shard_map/all_to_all | solution.py:299
  57.4 0.0 collective-permute-done.3.three_ref
  57.4 0.0 collective-permute-done.2.two_ref
  57.4 0.0 collective-permute-done.1.one_ref
  57.4 0.1 shard_map.90.own_ref
  57.5 0.0 copy-start.1
  57.5 2.1 %collective-permute-start.4 = (f32[584,128]{1,0:T(8,128)S(1)}, f32[584,128]{1,0:T(8,128)S(1)}, u32[]{:S(2)}, u32[]{:S(2)}) collective-permute-start(f32[584,128]{1,0:T(8,128)S(1)} %shard_map.90.own_ref), channel_id=1, source_target_pairs={{0,1},{1,0},{2,3},{3,2},{4,5},{5,4},{6,7},{7,6},{8,9},{9,8},{10,11... | collective-permute-start | bytes 897032 | tf_op jit(solution)/shard_map/ppermute | solution.py:360
  59.6 10.7 %all-to-all-done.2 = f32[16,1,1152]{2,1,0:T(1,128)S(1)} async-done(((f32[16,1,1152]{2,1,0:T(1,128)}), f32[16,1,1152]{2,1,0:T(1,128)S(1)}, u32[]{:S(2)}, u32[]{:S(2)}) %all-to-all-start.2) | async-done | bytes 73760 | tf_op jit(solution)/shard_map/all_to_all | solution.py:299
  70.3 0.8 shard_map.87
  71.0 3.5 %all-to-all-start.3 = ((f32[4,144,128]{2,1,0:T(8,128)}), f32[4,144,128]{2,1,0:T(8,128)S(1)}, u32[]{:S(2)}, u32[]{:S(2)}) async-start(f32[4,144,128]{2,1,0:T(8,128)} %shard_map.87), calls=%async_computation.3 | async-start | bytes 589824 | tf_op jit(solution)/shard_map/all_to_all | solution.py:299
  74.5 0.0 collective-permute-done.4.other_ref
  74.5 1.3 %shard_map.91 = (f32[36,64,64]{2,1,0:T(8,128)}, f32[4,64]{1,0:T(4,128)}) custom-call(f32[584,128]{1,0:T(8,128)S(1)} %shard_map.90.own_ref, f32[584,128]{1,0:T(8,128)S(1)} %collective-permute-done.4.other_ref), custom_call_target="tpu_custom_call" | custom-call | bytes 1188864 | tf_op jit(solution)/shard_map/pallas_call | solution.py:286
  75.8 5.6 %all-to-all-done.3.in_ref = f32[4,144,128]{2,1,0:T(8,128)S(1)} async-done(((f32[4,144,128]{2,1,0:T(8,128)}), f32[4,144,128]{2,1,0:T(8,128)S(1)}, u32[]{:S(2)}, u32[]{:S(2)}) %all-to-all-start.3) | async-done | bytes 294944 | tf_op jit(solution)/shard_map/all_to_all | solution.py:299
  81.3 0.0 copy-done.1
  81.3 0.9 %shard_map.88 = (f32[24,1536]{1,0:T(8,128)}, f32[24,1536]{1,0:T(8,128)}) custom-call(f32[4,144,128]{2,1,0:T(8,128)S(1)} %all-to-all-done.3.in_ref, f32[24,1536]{1,0:T(8,128)S(1)} %bitcast.13), custom_call_target="tpu_custom_call" | custom-call | bytes 737280 | tf_op jit(solution)/shard_map/pallas_call | solution.py:286
  (1 shorter events, 0.0 us)
Async XLA Ops:
  6.4 27.6 %copy-start = (f32[584,128]{1,0:T(8,128)S(1)}, f32[584,128]{1,0:T(8,128)}, u32[]{:S(2)}) copy-start(f32[584,128]{1,0:T(8,128)} %get-tuple-element.14.keep_ref) | copy-start | bytes 897028
  6.4 11.6 %all-to-all-start = ((f32[4,152,128]{2,1,0:T(8,128)}), f32[4,152,128]{2,1,0:T(8,128)S(1)}, u32[]{:S(2)}, u32[]{:S(2)}) async-start(f32[4,152,128]{2,1,0:T(8,128)} %get-tuple-element.11), calls=%async_computation | async-start | bytes 622592 | tf_op jit(solution)/shard_map/all_to_all | solution.py:299
  10.8 23.1 %collective-permute-start = (f32[584,128]{1,0:T(8,128)}, f32[584,128]{1,0:T(8,128)S(1)}, u32[]{:S(2)}, u32[]{:S(2)}) collective-permute-start(f32[584,128]{1,0:T(8,128)} %get-tuple-element.15), channel_id=1, source_target_pairs={{0,1},{1,0},{2,3},{3,2},{4,5},{5,4},{6,7},{7,6},{8,9},{9,8},{10,11... | collective-permute-start | bytes 897032 | tf_op jit(solution)/shard_map/ppermute | solution.py:344
  18.7 28.3 %all-to-all-start.1 = ((f32[16,1,1280]{2,1,0:T(1,128)}), f32[16,1,1280]{2,1,0:T(1,128)S(1)}, u32[]{:S(2)}, u32[]{:S(2)}) async-start(f32[16,1,1280]{2,1,0:T(1,128)} %bitcast.3), calls=%async_computation.1 | async-start | bytes 163840 | tf_op jit(solution)/shard_map/all_to_all | solution.py:299
  34.0 23.4 %collective-permute-start.3 = (f32[584,128]{1,0:T(8,128)S(1)}, f32[584,128]{1,0:T(8,128)S(1)}, u32[]{:S(2)}, u32[]{:S(2)}) collective-permute-start(f32[584,128]{1,0:T(8,128)S(1)} %shard_map.89.own_ref), channel_id=1, source_target_pairs={{0,6},{1,7},{2,0},{3,1},{4,2},{5,3},{6,4},{7,5},{8,14},{9,15},{10,... | collective-permute-start | bytes 897032 | tf_op jit(solution)/shard_map/ppermute | solution.py:351
  36.4 21.0 %collective-permute-start.2 = (f32[584,128]{1,0:T(8,128)S(1)}, f32[584,128]{1,0:T(8,128)S(1)}, u32[]{:S(2)}, u32[]{:S(2)}) collective-permute-start(f32[584,128]{1,0:T(8,128)S(1)} %shard_map.89.own_ref), channel_id=1, source_target_pairs={{0,4},{1,5},{2,6},{3,7},{4,0},{5,1},{6,2},{7,3},{8,12},{9,13},{10,... | collective-permute-start | bytes 897032 | tf_op jit(solution)/shard_map/ppermute | solution.py:351
  40.9 16.5 %collective-permute-start.1 = (f32[584,128]{1,0:T(8,128)S(1)}, f32[584,128]{1,0:T(8,128)S(1)}, u32[]{:S(2)}, u32[]{:S(2)}) collective-permute-start(f32[584,128]{1,0:T(8,128)S(1)} %shard_map.89.own_ref), channel_id=1, source_target_pairs={{0,2},{1,3},{2,4},{3,5},{4,6},{5,7},{6,0},{7,1},{8,10},{9,11},{10,... | collective-permute-start | bytes 897032 | tf_op jit(solution)/shard_map/ppermute | solution.py:351
  47.7 22.6 %all-to-all-start.2 = ((f32[16,1,1152]{2,1,0:T(1,128)}), f32[16,1,1152]{2,1,0:T(1,128)S(1)}, u32[]{:S(2)}, u32[]{:S(2)}) async-start(f32[16,1,1152]{2,1,0:T(1,128)} %bitcast.5), calls=%async_computation.2 | async-start | bytes 147456 | tf_op jit(solution)/shard_map/all_to_all | solution.py:299
  57.5 23.8 %copy-start.1 = (f32[1,1,24,1536]{3,2,1,0:T(8,128)S(1)}, f32[1,1,24,1536]{3,2,1,0:T(8,128)}, u32[]{:S(2)}) copy-start(f32[1,1,24,1536]{3,2,1,0:T(8,128)} %param.5) | copy-start | bytes 442372
  57.5 17.0 %collective-permute-start.4 = (f32[584,128]{1,0:T(8,128)S(1)}, f32[584,128]{1,0:T(8,128)S(1)}, u32[]{:S(2)}, u32[]{:S(2)}) collective-permute-start(f32[584,128]{1,0:T(8,128)S(1)} %shard_map.90.own_ref), channel_id=1, source_target_pairs={{0,1},{1,0},{2,3},{3,2},{4,5},{5,4},{6,7},{7,6},{8,9},{9,8},{10,11... | collective-permute-start | bytes 897032 | tf_op jit(solution)/shard_map/ppermute | solution.py:360
  71.0 10.3 %all-to-all-start.3 = ((f32[4,144,128]{2,1,0:T(8,128)}), f32[4,144,128]{2,1,0:T(8,128)S(1)}, u32[]{:S(2)}, u32[]{:S(2)}) async-start(f32[4,144,128]{2,1,0:T(8,128)} %shard_map.87), calls=%async_computation.3 | async-start | bytes 589824 | tf_op jit(solution)/shard_map/all_to_all | solution.py:299

commit v4 on v3

--- a/solution.py
+++ b/solution.py
@@ -201,12 +201,8 @@
         )
 
 
-def keep_kernel(keep_ref, got_ref, out_ref):
-    out_ref[...] = keep_ref[...] + got_ref[...]
-
-
-def total_kernel(scale, own_ref, one_ref, two_ref, three_ref, out_ref):
-    out_ref[...] = ((own_ref[...] + two_ref[...]) + (one_ref[...] + three_ref[...])) * scale
+def add_kernel(scale, own_ref, other_ref, out_ref):
+    out_ref[...] = (own_ref[...] + other_ref[...]) * scale
 
 
 def spread_kernel(depth_count, own_ref, other_ref, grad_ref, bias_ref):
@@ -342,13 +338,10 @@
     )
     came = exchange(send, rows)
     got = lax.ppermute(give, "dp", swap)
-    (mine,) = call(keep_kernel, [half], keep, got)
+    (mine,) = call(functools.partial(add_kernel, 1.0), [half], keep, got)
     (totals,) = call(functools.partial(compose_kernel, count), [((10 * count, 128), F32)], came)
     column = exchange(totals, columns)
-    ring = []
-    for hop in range(1, 4):
-        path = [(i, (i + 2 * hop) % parts) for i in range(parts)]
-        ring.append(lax.ppermute(mine, "dp", path))
+    got = lax.ppermute(mine, "dp", [(i, i ^ 2) for i in range(parts)])
     (before,) = call(
         functools.partial(scan_kernel, count),
         [((9 * count, 128), F32)],
@@ -356,7 +349,9 @@
         scratch=(pltpu.VMEM((count, 128), F32), pltpu.VMEM((count, 128), F32)),
     )
     home = exchange(before, columns)
-    (mine,) = call(functools.partial(total_kernel, 1.0 / parts), [half], mine, *ring)
+    (mine,) = call(functools.partial(add_kernel, 1.0), [half], mine, got)
+    got = lax.ppermute(mine, "dp", [(i, i ^ 4) for i in range(parts)])
+    (mine,) = call(functools.partial(add_kernel, 1.0 / parts), [half], mine, got)
     theirs = lax.ppermute(mine, "dp", swap)
     (spread,) = call(
         functools.partial(expand_kernel, count),

time: 82.8 us -> 78.4 us (0.947)
  starting transfers between devices: 47.4 us -> 38 us
  blocking collectives: 0 us -> 9.2 us
  waiting for transfers between devices: 23.9 us -> 19.5 us
  local copies, waits for them, and re-layouts: 0.01 us -> 0.97 us
    all_to_all x4 -> x3, starting transfers between devices: 32.8 us -> 23.1 us  [exchange(): lax.all_to_all(array.reshape(count, -1, 128) if array.ndim == 3 else arra...]
    all_to_all x0 -> x1, blocking collectives: none -> 9.2 us  [exchange(): lax.all_to_all(array.reshape(count, -1, 128) if array.ndim == 3 else arra...]
    all_to_all x4 -> x3, waiting for transfers between devices: 23.8 us -> 19.5 us  [exchange(): lax.all_to_all(array.reshape(count, -1, 128) if array.ndim == 3 else arra...]
    unnamed x4, local copies, waits for them, and re-layouts: 0.01 us -> 0.97 us
    pallas_call x8 -> x9, Pallas kernels: 10.2 us -> 9.48 us  [call(): pl.pallas_call(kernel, out_shape=shapes, in_specs=[far if i in anywhere e...]
    ppermute x3 -> x2, starting transfers between devices: 10.6 us -> 11.1 us  [the longest x1 6.87 us: body(): got = lax.ppermute(mine, 'dp', [(i, i ^ 2) for i in range(parts)])]
  transfers between devices with their start and end apart: 9 -> 7, of which waited for: 4 -> 2; matrix products, arithmetic and copies ran while one was open for 0% -> 0% of each run, Pallas kernels for 4% -> 3%
where the time goes in v4:
time: 78.4 us; the launch traced here: 77.9 us
  starting transfers between devices  38 us (48%)
  waiting for transfers between devices  19.5 us (25%)
  Pallas kernels  9.48 us (12%)
  blocking collectives  9.2 us (12%)
  local copies, waits for them, and re-layouts  0.97 us (1%)
    all_to_all x3, starting transfers between devices, exchange(): lax.all_to_all(array.reshape(count, -1, 128) if array.ndim == 3 else arra...  23.1 us
    all_to_all x3, waiting for transfers between devices, exchange(): lax.all_to_all(array.reshape(count, -1, 128) if array.ndim == 3 else arra...  19.5 us
    pallas_call x9, Pallas kernels, call(): pl.pallas_call(kernel, out_shape=shapes, in_specs=[far if i in anywhere e...  9.48 us
    all_to_all x1, blocking collectives, exchange(): lax.all_to_all(array.reshape(count, -1, 128) if array.ndim == 3 else arra...  9.2 us
    ppermute x1, starting transfers between devices, body(): got = lax.ppermute(mine, 'dp', [(i, i ^ 2) for i in range(parts)])  6.87 us
    ppermute x1, starting transfers between devices, body(): got = lax.ppermute(mine, 'dp', [(i, i ^ 4) for i in range(parts)])  4.2 us
    ppermute x1, starting transfers between devices, body(): theirs = lax.ppermute(mine, 'dp', swap)  1.92 us
    ppermute x1, starting transfers between devices, body(): got = lax.ppermute(give, 'dp', swap)  1.92 us
  transfers between devices with their start and end apart: 7, of which 2 were waited for; matrix products, arithmetic and copies ran while one was open for 0% of the time, Pallas kernels for 3%

profile of v4, /device:TPU:8, one launch (start us, length us, event | category | flops | bytes accessed | tf_op | source)
XLA Modules:
  0.0 77.9 jit_solution(124775376640097056)
XLA Ops:
  0.6 5.7 %shard_map.84 = (f32[4,152,128]{2,1,0:T(8,128)}, f32[584,128]{1,0:T(8,128)}, f32[584,128]{1,0:T(8,128)}) custom-call(f32[24,1536]{1,0:T(8,128)} %bitcast.12, f32[24,1536]{1,0:T(8,128)} %bitcast.16, bf16[36,64,64]{2,1,0:T(8,128)(2,1)} %bitcast.15, f32[4,64]{1,0:T(4,128)} %b_hbm.1, f32[1,64]{1,0:T(1,128)} %g_hbm.1), custom_call_target="tpu_custom_call" | custom-call | flops 679477248 | bytes 1500416 | tf_op jit(solution)/shard_map/pallas_call | solution.py:282
  6.3 1.9 %collective-permute-start = (f32[584,128]{1,0:T(8,128)}, f32[584,128]{1,0:T(8,128)S(1)}, u32[]{:S(2)}, u32[]{:S(2)}) collective-permute-start(f32[584,128]{1,0:T(8,128)} %get-tuple-element.15), channel_id=1, source_target_pairs={{0,1},{1,0},{2,3},{3,2},{4,5},{5,4},{6,7},{7,6},{8,9},{9,8},{10,11... | collective-permute-start | bytes 897032 | tf_op jit(solution)/shard_map/ppermute | solution.py:340
  8.3 4.3 %all-to-all-start = ((f32[4,152,128]{2,1,0:T(8,128)}), f32[4,152,128]{2,1,0:T(8,128)S(1)}, u32[]{:S(2)}, u32[]{:S(2)}) async-start(f32[4,152,128]{2,1,0:T(8,128)} %get-tuple-element.11), calls=%async_computation | async-start | bytes 622592 | tf_op jit(solution)/shard_map/all_to_all | solution.py:295
  12.6 0.0 collective-permute-done.other_ref
  12.6 0.0 copy-start
  12.6 1.0 %copy-done = f32[584,128]{1,0:T(8,128)S(1)} copy-done((f32[584,128]{1,0:T(8,128)S(1)}, f32[584,128]{1,0:T(8,128)}, u32[]{:S(2)}) %copy-start) | copy-done | bytes 299032
  13.6 6.9 %collective-permute-start.1 = (f32[584,128]{1,0:T(8,128)S(1)}, f32[584,128]{1,0:T(8,128)S(1)}, u32[]{:S(2)}, u32[]{:S(2)}) collective-permute-start(f32[584,128]{1,0:T(8,128)S(1)} %shard_map.89.own_ref), channel_id=1, source_target_pairs={{0,2},{1,3},{2,0},{3,1},{4,6},{5,7},{6,4},{7,5},{8,10},{9,11},{10,... | collective-permute-start | bytes 897032 | tf_op jit(solution)/shard_map/ppermute | solution.py:344
  20.5 0.0 all-to-all-done.in_ref.came_ref
  20.5 0.7 shard_map.85
  21.2 15.1 %all-to-all-start.1 = ((f32[16,1,1280]{2,1,0:T(1,128)}), f32[16,1,1280]{2,1,0:T(1,128)S(1)}, u32[]{:S(2)}, u32[]{:S(2)}) async-start(f32[16,1,1280]{2,1,0:T(1,128)} %bitcast.3), calls=%async_computation.1 | async-start | bytes 163840 | tf_op jit(solution)/shard_map/all_to_all | solution.py:295
  36.4 0.0 collective-permute-done.1.other_ref
  36.4 4.2 %collective-permute-start.2 = (f32[584,128]{1,0:T(8,128)S(1)}, f32[584,128]{1,0:T(8,128)S(1)}, u32[]{:S(2)}, u32[]{:S(2)}) collective-permute-start(f32[584,128]{1,0:T(8,128)S(1)} %shard_map.90.own_ref), channel_id=1, source_target_pairs={{0,4},{1,5},{2,6},{3,7},{4,0},{5,1},{6,2},{7,3},{8,12},{9,13},{10,... | collective-permute-start | bytes 897032 | tf_op jit(solution)/shard_map/ppermute | solution.py:353
  40.6 8.6 %all-to-all-done.1 = f32[16,1,1280]{2,1,0:T(1,128)S(1)} async-done(((f32[16,1,1280]{2,1,0:T(1,128)}), f32[16,1,1280]{2,1,0:T(1,128)S(1)}, u32[]{:S(2)}, u32[]{:S(2)}) %all-to-all-start.1) | async-done | bytes 81952 | tf_op jit(solution)/shard_map/all_to_all | solution.py:295
  49.2 0.7 shard_map.86
  49.9 0.0 copy-start.1
  49.9 3.6 %all-to-all-start.2 = ((f32[16,1,1152]{2,1,0:T(1,128)}), f32[16,1,1152]{2,1,0:T(1,128)S(1)}, u32[]{:S(2)}, u32[]{:S(2)}) async-start(f32[16,1,1152]{2,1,0:T(1,128)} %bitcast.5), calls=%async_computation.2 | async-start | bytes 147456 | tf_op jit(solution)/shard_map/all_to_all | solution.py:295
  53.6 0.0 collective-permute-done.2.other_ref
  53.6 1.9 %collective-permute-start.3 = (f32[584,128]{1,0:T(8,128)S(1)}, f32[584,128]{1,0:T(8,128)S(1)}, u32[]{:S(2)}, u32[]{:S(2)}) collective-permute-start(f32[584,128]{1,0:T(8,128)S(1)} %shard_map.91.own_ref), channel_id=1, source_target_pairs={{0,1},{1,0},{2,3},{3,2},{4,5},{5,4},{6,7},{7,6},{8,9},{9,8},{10,11... | collective-permute-start | bytes 897032 | tf_op jit(solution)/shard_map/ppermute | solution.py:355
  55.6 10.9 %all-to-all-done.2 = f32[16,1,1152]{2,1,0:T(1,128)S(1)} async-done(((f32[16,1,1152]{2,1,0:T(1,128)}), f32[16,1,1152]{2,1,0:T(1,128)S(1)}, u32[]{:S(2)}, u32[]{:S(2)}) %all-to-all-start.2) | async-done | bytes 73760 | tf_op jit(solution)/shard_map/all_to_all | solution.py:295
  66.4 0.1 shard_map.87
  66.5 9.2 %all_to_all.28.in_ref = f32[4,144,128]{2,1,0:T(8,128)S(1)} all-to-all(f32[4,144,128]{2,1,0:T(8,128)S(1)} %shard_map.87), channel_id=1, replica_groups={{0,8,16,24},{32,40,48,56},{64,72,80,88},{96,104,112,120},{128,136,144,1..., dimensions={0} | all-to-all | bytes 589824 | tf_op jit(solution)/shard_map/all_to_all | solution.py:295
  75.7 0.0 copy-done.1
  75.7 0.9 %shard_map.88 = (f32[24,1536]{1,0:T(8,128)}, f32[24,1536]{1,0:T(8,128)}) custom-call(f32[4,144,128]{2,1,0:T(8,128)S(1)} %all_to_all.28.in_ref, f32[24,1536]{1,0:T(8,128)S(1)} %bitcast.13), custom_call_target="tpu_custom_call" | custom-call | bytes 737280 | tf_op jit(solution)/shard_map/pallas_call | solution.py:282
  76.6 0.0 collective-permute-done.3.other_ref
  76.6 1.3 %shard_map.92 = (f32[36,64,64]{2,1,0:T(8,128)}, f32[4,64]{1,0:T(4,128)}) custom-call(f32[584,128]{1,0:T(8,128)S(1)} %shard_map.91.own_ref, f32[584,128]{1,0:T(8,128)S(1)} %collective-permute-done.3.other_ref), custom_call_target="tpu_custom_call" | custom-call | bytes 1188864 | tf_op jit(solution)/shard_map/pallas_call | solution.py:282
  (3 shorter events, 0.1 us)
Async XLA Ops:
  6.3 6.2 %collective-permute-start = (f32[584,128]{1,0:T(8,128)}, f32[584,128]{1,0:T(8,128)S(1)}, u32[]{:S(2)}, u32[]{:S(2)}) collective-permute-start(f32[584,128]{1,0:T(8,128)} %get-tuple-element.15), channel_id=1, source_target_pairs={{0,1},{1,0},{2,3},{3,2},{4,5},{5,4},{6,7},{7,6},{8,9},{9,8},{10,11... | collective-permute-start | bytes 897032 | tf_op jit(solution)/shard_map/ppermute | solution.py:340
  8.3 12.2 %all-to-all-start = ((f32[4,152,128]{2,1,0:T(8,128)}), f32[4,152,128]{2,1,0:T(8,128)S(1)}, u32[]{:S(2)}, u32[]{:S(2)}) async-start(f32[4,152,128]{2,1,0:T(8,128)} %get-tuple-element.11), calls=%async_computation | async-start | bytes 622592 | tf_op jit(solution)/shard_map/all_to_all | solution.py:295
  12.6 1.0 %copy-start = (f32[584,128]{1,0:T(8,128)S(1)}, f32[584,128]{1,0:T(8,128)}, u32[]{:S(2)}) copy-start(f32[584,128]{1,0:T(8,128)} %get-tuple-element.14.own_ref) | copy-start | bytes 897028
  13.6 22.8 %collective-permute-start.1 = (f32[584,128]{1,0:T(8,128)S(1)}, f32[584,128]{1,0:T(8,128)S(1)}, u32[]{:S(2)}, u32[]{:S(2)}) collective-permute-start(f32[584,128]{1,0:T(8,128)S(1)} %shard_map.89.own_ref), channel_id=1, source_target_pairs={{0,2},{1,3},{2,0},{3,1},{4,6},{5,7},{6,4},{7,5},{8,10},{9,11},{10,... | collective-permute-start | bytes 897032 | tf_op jit(solution)/shard_map/ppermute | solution.py:344
  21.2 28.0 %all-to-all-start.1 = ((f32[16,1,1280]{2,1,0:T(1,128)}), f32[16,1,1280]{2,1,0:T(1,128)S(1)}, u32[]{:S(2)}, u32[]{:S(2)}) async-start(f32[16,1,1280]{2,1,0:T(1,128)} %bitcast.3), calls=%async_computation.1 | async-start | bytes 163840 | tf_op jit(solution)/shard_map/all_to_all | solution.py:295
  36.4 17.1 %collective-permute-start.2 = (f32[584,128]{1,0:T(8,128)S(1)}, f32[584,128]{1,0:T(8,128)S(1)}, u32[]{:S(2)}, u32[]{:S(2)}) collective-permute-start(f32[584,128]{1,0:T(8,128)S(1)} %shard_map.90.own_ref), channel_id=1, source_target_pairs={{0,4},{1,5},{2,6},{3,7},{4,0},{5,1},{6,2},{7,3},{8,12},{9,13},{10,... | collective-permute-start | bytes 897032 | tf_op jit(solution)/shard_map/ppermute | solution.py:353
  49.9 25.8 %copy-start.1 = (f32[1,1,24,1536]{3,2,1,0:T(8,128)S(1)}, f32[1,1,24,1536]{3,2,1,0:T(8,128)}, u32[]{:S(2)}) copy-start(f32[1,1,24,1536]{3,2,1,0:T(8,128)} %param.5) | copy-start | bytes 442372
  49.9 16.5 %all-to-all-start.2 = ((f32[16,1,1152]{2,1,0:T(1,128)}), f32[16,1,1152]{2,1,0:T(1,128)S(1)}, u32[]{:S(2)}, u32[]{:S(2)}) async-start(f32[16,1,1152]{2,1,0:T(1,128)} %bitcast.5), calls=%async_computation.2 | async-start | bytes 147456 | tf_op jit(solution)/shard_map/all_to_all | solution.py:295
  53.6 23.0 %collective-permute-start.3 = (f32[584,128]{1,0:T(8,128)S(1)}, f32[584,128]{1,0:T(8,128)S(1)}, u32[]{:S(2)}, u32[]{:S(2)}) collective-permute-start(f32[584,128]{1,0:T(8,128)S(1)} %shard_map.91.own_ref), channel_id=1, source_target_pairs={{0,1},{1,0},{2,3},{3,2},{4,5},{5,4},{6,7},{7,6},{8,9},{9,8},{10,11... | collective-permute-start | bytes 897032 | tf_op jit(solution)/shard_map/ppermute | solution.py:355
